TPU v7x, 256 devices: a whole 4x4x8 slice. The times are simulated.
256 devices in a mesh: row: 64 (over z, x, core), col: 4 (over y).
Axes of the slice: x: 4, y: 4, z: 8, core: 2. Of those that a mesh axis runs over, the one named last changes fastest.
Arguments:
- right_sides: float32 [4, 256, 128, 128], P(None, 'row'), may hold values from -6 to 6
- inverse_diag: float32 [4, 256, 128, 128], P(None, 'row', 'col'), may hold values from -1 to 2
- lower_blocks: float32 [3, 256, 16, 128, 128], P(None, 'row', None, 'col'), may hold values from -0.09375 to 0.09375
- depends_on: int32 [3, 256, 16], replicated, may hold values from 0 to 255, as said below
Outputs:
- solution: float32 [4, 256, 128, 128], P(None, 'row', 'col')
Inputs may be any that keep to these rules, and one draw needn't show every extreme that they name: `depends_on`: in each level, the supernodes of one device along row name the supernodes of any one device along row at most 2 times in all, and some pair of devices reaches 2 in every level.
All inputs are finite; a program needn't handle non-finite values.
Results may differ from a plain program's by a relative error of at most 0.0001.
Values sent between devices are 32-bit elements; how exact they have to be, the bound alone decides.
A program may use at most 64 MiB of HBM per device.

v0:
```python
import jax
import jax.numpy as jnp
from jax import lax
from jax.sharding import PartitionSpec as P

exact_mode = lax.Precision.HIGHEST


def fetch_blocks(previous, wanted):
    shard_rows = lax.all_gather(previous, "row", axis=0, tiled=True)
    chooser = (wanted[:, None] == jnp.arange(shard_rows.shape[0], dtype=jnp.int32)[None, :]).astype(
        jnp.float32
    )
    return jnp.einsum("en,nrk->erk", chooser, shard_rows, precision=exact_mode)


def return_terms(terms, wanted, local_count):
    owners = (
        jnp.arange(local_count * lax.axis_size("row"), dtype=jnp.int32)[:, None] == wanted[None, :]
    ).astype(jnp.float32)
    return lax.psum_scatter(
        jnp.einsum("me,erk->mrk", owners, terms, precision=exact_mode),
        "row",
        scatter_dimension=0,
        tiled=True,
    )


def forward_update(partial_value):
    return lax.psum(partial_value, "col")


def backward_solve(inverse_level, rest):
    partial_value = jnp.einsum("jab,jak->jbk", inverse_level, rest, precision=exact_mode)
    return lax.psum(partial_value, "col")


def on_device(right_sides, inverse_diag, lower_blocks, depends_on):
    levels, local_count, width, columns = right_sides.shape
    share = inverse_diag.shape[2]
    fan_in = lower_blocks.shape[2]
    my_row = lax.axis_index("row")
    my_col = lax.axis_index("col")
    entries = local_count * fan_in
    wanted_all = [
        lax.dynamic_slice_in_dim(
            depends_on[level_no], my_row * local_count, local_count, 0
        ).reshape(entries)
        for level_no in range(levels - 1)
    ]
    solved_here = [
        jnp.einsum("jab,jbk->jak", inverse_diag[0], right_sides[0], precision=exact_mode)
    ]
    for level_no in range(1, levels):
        picked = fetch_blocks(solved_here[-1], wanted_all[level_no - 1])
        partial_value = jnp.einsum(
            "jdba,jdbk->jak",
            lower_blocks[level_no - 1],
            picked.reshape(local_count, fan_in, share, columns),
            precision=exact_mode,
        )
        update = forward_update(partial_value)
        residual = right_sides[level_no] - update
        solved_here.append(
            jnp.einsum("jab,jbk->jak", inverse_diag[level_no], residual, precision=exact_mode)
        )
    full_sol = backward_solve(inverse_diag[levels - 1], solved_here[levels - 1])
    pieces = [lax.dynamic_slice_in_dim(full_sol, my_col * share, share, 1)]
    for level_no in range(levels - 2, -1, -1):
        terms = jnp.einsum(
            "jdba,jak->jdbk", lower_blocks[level_no], full_sol, precision=exact_mode
        ).reshape(entries, share, columns)
        returned = return_terms(terms, wanted_all[level_no], local_count)
        rest = solved_here[level_no] - returned
        full_sol = backward_solve(inverse_diag[level_no], rest)
        pieces.insert(0, lax.dynamic_slice_in_dim(full_sol, my_col * share, share, 1))
    return jnp.stack(pieces)


def solution(mesh):
    return jax.shard_map(
        on_device,
        mesh=mesh,
        in_specs=(
            P(None, "row", None, None),
            P(None, "row", "col", None),
            P(None, "row", None, "col", None),
            P(),
        ),
        out_specs=P(None, "row", "col", None),
        check_vma=False,
    )
```

profile of v0, /device:TPU:2, one launch (start us, length us, event | category | flops | bytes accessed | tf_op | source)
XLA Modules:
  0.0 1079.7 jit_solution(4726448590712107465)
XLA Ops:
  9.6 3.6 fusion.65
  13.2 77.8 %all-gather.4.cloned.1.call-done = f32[256,32,128]{2,1,0:T(8,128)} async-done(((f32[4,32,128]{2,1,0:T(8,128)}), f32[256,32,128]{2,1,0:T(8,128)}) %all-gather.4.cloned.1.call-update) | async-done | bytes 4194320 | tf_op jit(solution)/shard_map/all_gather | solution.py:10
  91.0 6.2 fusion.4
  97.2 3.0 convolution_bitcast_fusion.6
  101.2 44.4 %all-reduce.8.cloned.1.call-done = f32[4,128,128]{1,2,0:T(8,128)} async-done(((f32[4,128,128]{1,2,0:T(8,128)}), f32[4,128,128]{1,2,0:T(8,128)}) %all-reduce.8.cloned.1.call-update) | async-done | bytes 262160 | tf_op jit(solution)/shard_map/psum | solution.py:30
  145.6 2.1 convolution_bitcast_fusion.8
  148.3 78.8 %all-gather.6.cloned.1.call-done = f32[256,32,128]{2,1,0:T(8,128)} async-done(((f32[4,32,128]{2,1,0:T(8,128)}), f32[256,32,128]{2,1,0:T(8,128)}) %all-gather.6.cloned.1.call-update) | async-done | bytes 4194320 | tf_op jit(solution)/shard_map/all_gather | solution.py:10
  227.1 6.1 fusion.2
  233.2 3.0 convolution_bitcast_fusion.5
  236.4 45.2 %all-reduce.10.cloned.1.call-done = f32[4,128,128]{1,2,0:T(8,128)} async-done(((f32[4,128,128]{1,2,0:T(8,128)}), f32[4,128,128]{1,2,0:T(8,128)}) %all-reduce.10.cloned.1.call-update) | async-done | bytes 262160 | tf_op jit(solution)/shard_map/psum | solution.py:30
  281.6 2.1 convolution_bitcast_fusion.7
  284.3 78.3 %all-gather.8.cloned.1.call-done = f32[256,32,128]{2,1,0:T(8,128)} async-done(((f32[4,32,128]{2,1,0:T(8,128)}), f32[256,32,128]{2,1,0:T(8,128)}) %all-gather.8.cloned.1.call-update) | async-done | bytes 4194320 | tf_op jit(solution)/shard_map/all_gather | solution.py:10
  362.6 6.1 fusion
  368.7 4.4 convolution_bitcast_fusion.4
  375.0 43.5 %all-reduce.12.cloned.1.call-done = f32[4,128,128]{1,2,0:T(8,128)} async-done(((f32[4,128,128]{1,2,0:T(8,128)}), f32[4,128,128]{1,2,0:T(8,128)}) %all-reduce.12.cloned.1.call-update) | async-done | bytes 262160 | tf_op jit(solution)/shard_map/psum | solution.py:30
  422.0 46.8 %all-reduce.14.cloned.1.call-done = f32[4,128,128]{1,2,0:T(8,128)} async-done(((f32[4,128,128]{1,2,0:T(8,128)}), f32[4,128,128]{1,2,0:T(8,128)}) %all-reduce.14.cloned.1.call-update) | async-done | bytes 262160 | tf_op jit(solution)/shard_map/psum | solution.py:35
  470.8 2.3 fusion.16
  473.1 4.4 copy.45
  477.6 143.6 %reduce-scatter.4.cloned.1.call-done = f32[4,32,128]{2,1,0:T(8,128)} async-done(((f32[256,32,128]{2,1,0:T(8,128)}), f32[4,32,128]{2,1,0:T(8,128)}) %reduce-scatter.4.cloned.1.call-update) | async-done | bytes 65552 | tf_op jit(solution)/shard_map/reduce_scatter | solution.py:21
  621.1 2.1 convolution_bitcast_fusion.2
  623.5 46.0 %all-reduce.16.cloned.1.call-done = f32[4,128,128]{1,2,0:T(8,128)} async-done(((f32[4,128,128]{1,2,0:T(8,128)}), f32[4,128,128]{1,2,0:T(8,128)}) %all-reduce.16.cloned.1.call-update) | async-done | bytes 262160 | tf_op jit(solution)/shard_map/psum | solution.py:35
  669.6 1.9 fusion.8
  671.5 2.3 fusion.14
  673.9 4.4 copy.49
  678.3 143.5 %reduce-scatter.6.cloned.1.call-done = f32[4,32,128]{2,1,0:T(8,128)} async-done(((f32[256,32,128]{2,1,0:T(8,128)}), f32[4,32,128]{2,1,0:T(8,128)}) %reduce-scatter.6.cloned.1.call-update) | async-done | bytes 65552 | tf_op jit(solution)/shard_map/reduce_scatter | solution.py:21
  821.8 2.1 convolution_bitcast_fusion.1
  824.3 46.0 %all-reduce.18.cloned.1.call-done = f32[4,128,128]{1,2,0:T(8,128)} async-done(((f32[4,128,128]{1,2,0:T(8,128)}), f32[4,128,128]{1,2,0:T(8,128)}) %all-reduce.18.cloned.1.call-update) | async-done | bytes 262160 | tf_op jit(solution)/shard_map/psum | solution.py:35
  872.3 2.3 fusion.12
  874.6 4.4 copy.53
  879.1 143.5 %reduce-scatter.8.cloned.1.call-done = f32[4,32,128]{2,1,0:T(8,128)} async-done(((f32[256,32,128]{2,1,0:T(8,128)}), f32[4,32,128]{2,1,0:T(8,128)}) %reduce-scatter.8.cloned.1.call-update) | async-done | bytes 65552 | tf_op jit(solution)/shard_map/reduce_scatter | solution.py:21
  1022.6 2.1 convolution_bitcast_fusion
  1025.5 45.5 %all-reduce.20.cloned.1.call-done = f32[4,128,128]{1,2,0:T(8,128)} async-done(((f32[4,128,128]{1,2,0:T(8,128)}), f32[4,128,128]{1,2,0:T(8,128)}) %all-reduce.20.cloned.1.call-update) | async-done | bytes 262160 | tf_op jit(solution)/shard_map/psum | solution.py:35
  (73 shorter events, 17.9 us)
Async XLA Ops:
  6.5 84.4 %all-gather.4.cloned.1.call-start = ((), (), s32[]{:S(2)}) async-start(), calls=%async_computation.3 | async-start | bytes 4259840 | tf_op jit(solution)/shard_map/all_gather | solution.py:10
  8.5 137.1 %all-reduce.8.cloned.1.call-start = ((), (), s32[]{:S(2)}) async-start(), calls=%async_computation.4 | async-start | bytes 524288 | tf_op jit(solution)/shard_map/psum | solution.py:30
  13.2 87.1 %copy-start.5 = (f32[4,4,128,128]{3,2,1,0:T(8,128)S(1)}, f32[4,4,128,128]{3,2,1,0:T(8,128)}, u32[]{:S(2)}) copy-start(f32[4,4,128,128]{3,2,1,0:T(8,128)} %param.4) | copy-start | bytes 3145732
  91.0 6.2 copy-start.6
  97.2 48.4 %copy-start.4 = (f32[4,4,32,128]{3,2,1,0:T(8,128)S(1)}, f32[4,4,32,128]{3,2,1,0:T(8,128)}, u32[]{:S(2)}) copy-start(f32[4,4,32,128]{3,2,1,0:T(8,128)} %param.5) | copy-start | bytes 786436
  100.2 126.9 %all-gather.6.cloned.1.call-start = ((), (), s32[]{:S(2)}) async-start(), calls=%async_computation.5 | async-start | bytes 4259840 | tf_op jit(solution)/shard_map/all_gather | solution.py:10
  147.7 133.9 %all-reduce.10.cloned.1.call-start = ((), (), s32[]{:S(2)}) async-start(), calls=%async_computation.6 | async-start | bytes 524288 | tf_op jit(solution)/shard_map/psum | solution.py:30
  236.3 126.3 %all-gather.8.cloned.1.call-start = ((), (), s32[]{:S(2)}) async-start(), calls=%async_computation.7 | async-start | bytes 4259840 | tf_op jit(solution)/shard_map/all_gather | solution.py:10
  283.7 134.8 %all-reduce.12.cloned.1.call-start = ((), (), s32[]{:S(2)}) async-start(), calls=%async_computation.8 | async-start | bytes 524288 | tf_op jit(solution)/shard_map/psum | solution.py:30
  368.7 100.1 %copy-start = (f32[3,4,16,32,128]{4,3,2,1,0:T(8,128)S(1)}, f32[3,4,16,32,128]{4,3,2,1,0:T(8,128)}, u32[]{:S(2)}) copy-start(f32[3,4,16,32,128]{4,3,2,1,0:T(8,128)} %param.6) | copy-start | bytes 9437188
  373.1 95.7 %all-reduce.14.cloned.1.call-start = ((), (), s32[]{:S(2)}) async-start(), calls=%async_computation.9 | async-start | bytes 524288 | tf_op jit(solution)/shard_map/psum | solution.py:35
  421.4 199.7 %reduce-scatter.4.cloned.1.call-start = ((), (), s32[]{:S(2)}) async-start(), calls=%async_computation.10 | async-start | bytes 4259840 | tf_op jit(solution)/shard_map/reduce_scatter | solution.py:21
  477.5 143.6 %copy-start.8 = (f32[4,32,128]{2,1,0:T(8,128)S(1)}, f32[4,32,128]{2,1,0:T(8,128)}, u32[]{:S(2)}) copy-start(f32[4,32,128]{2,1,0:T(8,128)} %convolution_bitcast_fusion.7) | copy-start | bytes 196612
  477.5 192.0 %all-reduce.16.cloned.1.call-start = ((), (), s32[]{:S(2)}) async-start(), calls=%async_computation.11 | async-start | bytes 524288 | tf_op jit(solution)/shard_map/psum | solution.py:35
  623.3 198.6 %reduce-scatter.6.cloned.1.call-start = ((), (), s32[]{:S(2)}) async-start(), calls=%async_computation.12 | async-start | bytes 4259840 | tf_op jit(solution)/shard_map/reduce_scatter | solution.py:21
  678.2 143.6 %copy-start.7 = (f32[4,32,128]{2,1,0:T(8,128)S(1)}, f32[4,32,128]{2,1,0:T(8,128)}, u32[]{:S(2)}) copy-start(f32[4,32,128]{2,1,0:T(8,128)} %convolution_bitcast_fusion.8) | copy-start | bytes 196612
  678.3 192.0 %all-reduce.18.cloned.1.call-start = ((), (), s32[]{:S(2)}) async-start(), calls=%async_computation.13 | async-start | bytes 524288 | tf_op jit(solution)/shard_map/psum | solution.py:35
  824.0 198.6 %reduce-scatter.8.cloned.1.call-start = ((), (), s32[]{:S(2)}) async-start(), calls=%async_computation.14 | async-start | bytes 4259840 | tf_op jit(solution)/shard_map/reduce_scatter | solution.py:21
  879.0 143.6 %copy-start.9 = (f32[4,32,128]{2,1,0:T(8,128)S(1)}, f32[4,32,128]{2,1,0:T(8,128)}, u32[]{:S(2)}) copy-start(f32[4,32,128]{2,1,0:T(8,128)} %fusion.22) | copy-start | bytes 196612
  879.0 145.8 %copy-start.1 = (f32[4,128,128]{1,2,0:T(8,128)S(1)}, f32[4,128,128]{1,2,0:T(8,128)}, u32[]{:S(2)}) copy-start(f32[4,128,128]{1,2,0:T(8,128)} %all-reduce.14.cloned.1.call-done) | copy-start | bytes 786436
  879.0 146.0 %copy-start.2 = (f32[4,128,128]{1,2,0:T(8,128)S(1)}, f32[4,128,128]{1,2,0:T(8,128)}, u32[]{:S(2)}) copy-start(f32[4,128,128]{1,2,0:T(8,128)} %all-reduce.16.cloned.1.call-done) | copy-start | bytes 786436
  879.0 146.3 %copy-start.3 = (f32[4,128,128]{1,2,0:T(8,128)S(1)}, f32[4,128,128]{1,2,0:T(8,128)}, u32[]{:S(2)}) copy-start(f32[4,128,128]{1,2,0:T(8,128)} %all-reduce.18.cloned.1.call-done) | copy-start | bytes 786436
  879.0 192.0 %all-reduce.20.cloned.1.call-start = ((), (), s32[]{:S(2)}) async-start(), calls=%async_computation.15 | async-start | bytes 524288 | tf_op jit(solution)/shard_map/psum | solution.py:35
Sparse Core Ops, SparseCore 0:
  10.1 80.7 all-gather.3
  100.3 45.2 all-reduce.7
  148.7 78.3 all-gather.5
  236.4 45.1 all-reduce.9
  284.2 78.3 all-gather.7
  373.2 45.2 all-reduce.11
  421.5 47.2 all-reduce.13
  477.6 143.4 reduce-scatter.3
  623.6 45.9 all-reduce.15
  678.4 143.4 reduce-scatter.5
  824.3 45.9 all-reduce.17
  879.1 143.4 reduce-scatter.7
  1025.0 45.9 all-reduce.19
where the time goes:
time: 1090 us; the launch traced here: 1080 us
  waiting for transfers between devices  983 us (90%)
  matrix products  57.1 us (5%)
  local copies, waits for them, and re-layouts  22.8 us (2%)
  between operations  13.7 us (1%)
    reduce_scatter x3, waiting for transfers between devices, return_terms(): lax.psum_scatter(jnp.einsum('me,erk->mrk', owners, terms, precision=exact...  431 us
    all_gather x3, waiting for transfers between devices, fetch_blocks(): shard_rows = lax.all_gather(previous, 'row', axis=0, tiled=True)  235 us
    psum x4, waiting for transfers between devices, backward_solve(): return lax.psum(partial_value, 'col')  184 us
    psum x3, waiting for transfers between devices, forward_update(): return lax.psum(partial_value, 'col')  133 us
  transfers between devices with their start and end apart: 13, of which 13 were waited for; matrix products, arithmetic and copies ran while one was open for 1% of the time, Pallas kernels for 0%

commit v1 on v0

v1 whole, which is shorter than its diff:
```python
import jax
import jax.numpy as jnp
from jax import lax
from jax.experimental import pallas as pl
from jax.experimental.pallas import tpu as pltpu
from jax.sharding import PartitionSpec as P

MESH = pl.DeviceIdType.MESH
EXACT = lax.Precision.HIGHEST
NZ, NX = 8, 4
X_POS = {0: 0, 1: 1, 3: 2, 2: 3}
Z_POS = {0: 0, 1: 1, 7: 2, 2: 3, 6: 4, 3: 5, 5: 6, 4: 7}
GROUPS = [(0, 1), (1, 2), (3, 2), (5, 2), (7, 1)]


def exact_dot(a, b):
    return jnp.dot(a, b, precision=EXACT, preferred_element_type=jnp.float32)


def ring_pos(distance, size):
    return jnp.where(
        distance == 0,
        0,
        jnp.where(distance <= size // 2, 2 * distance - 1, 2 * (size - distance)),
    )


def block_place(block, z_of, x_of):
    owner, local = block // 4, block % 4
    a = z_of(owner // (2 * NX)) % NZ
    b = x_of(owner // 2 % NX) % NX
    slot_a = a * NX + ring_pos(b, NX)
    slot_b = ring_pos(b, NX) * NZ + ring_pos(a, NZ)
    return jnp.where(local < 2, 2 * slot_a, 64 + 2 * slot_b) + local % 2, owner % 2


def kernel(
    fwd_idx, bwd_idx, rhs_hbm, inv_hbm, low_hbm, out_ref,
    rhs, inv, low, low_t, fwd, own_part, gath_0, gath_1, gath_2, part, col_in, rest,
    sol, terms_0, terms_1, terms_2, own, up_a, dn_a, row_x, in_x, mid_l, mid_r, fin_l, fin_r, col_z, up_z, dn_z,
    load_sem, send_sem, inv_sem, ag_sem, rs_sem, col_sem,
):
    gath, terms = (gath_0, gath_1, gath_2), (terms_0, terms_1, terms_2)
    row, c = lax.axis_index("row"), lax.axis_index("col")
    z, x, core = row // (2 * NX), row // 2 % NX, row % 2

    def at_row(zz, xx, cc):
        return ((zz * NX + xx) * 2 + cc, c)

    z_up, z_dn = at_row((z + 1) % NZ, x, core), at_row((z + NZ - 1) % NZ, x, core)
    x_rt, x_lf = at_row(z, (x + 1) % NX, core), at_row(z, (x + NX - 1) % NX, core)
    x_far = at_row(z, (x + 2) % NX, core)
    sib = at_row(z, x, 1 - core)
    col_dev = [None] + [(row, (c + t) % 4) for t in (1, 2, 3)]

    loads = [
        pltpu.make_async_copy(inv_hbm, inv.at[:, :, c], load_sem.at[0]),
        pltpu.make_async_copy(rhs_hbm.at[0], rhs.at[0], load_sem.at[1]),
        pltpu.make_async_copy(rhs_hbm.at[pl.ds(1, 3)], rhs.at[pl.ds(1, 3)], load_sem.at[2]),
        pltpu.make_async_copy(low_hbm, low, load_sem.at[3]),
    ]
    for load in loads:
        load.start()

    barrier = pltpu.get_barrier_semaphore()
    partners = [z_up, z_dn, x_rt, x_lf, x_far, sib] + col_dev[1:]
    for partner in partners:
        pl.semaphore_signal(barrier, inc=1, device_id=partner, device_id_type=MESH)

    for level in range(3):
        terms[level][128] = jnp.zeros((32, 128), jnp.float32)
    loads[0].wait()
    loads[1].wait()
    for j in range(4):
        fwd[0, j] = exact_dot(inv[0, j, c], rhs[0, j])
    pl.semaphore_wait(barrier, len(partners))

    def put(src, dst, sem, device, out_sem):
        pltpu.make_async_remote_copy(
            src_ref=src, dst_ref=dst, send_sem=out_sem, recv_sem=sem, device_id=device, device_id_type=MESH
        ).start()

    def take(dst, sem, device=None):
        pltpu.make_async_remote_copy(
            src_ref=dst, dst_ref=dst, send_sem=send_sem.at[0], recv_sem=sem, device_id=sib, device_id_type=MESH
        ).wait_recv()

    def sent(count, out_sem):
        ref = gath[0].at[pl.ds(0, count)]
        pltpu.make_async_remote_copy(
            src_ref=ref, dst_ref=ref, send_sem=out_sem, recv_sem=out_sem, device_id=sib, device_id_type=MESH
        ).wait_send()

    def gather_row(level, between):
        g_sem = send_sem.at[0]
        ids = {}

        def sem(key):
            return ag_sem.at[level, ids.setdefault(key, len(ids))]

        def ref_a(a, pos, count):
            return gath[level].at[pl.ds(2 * (a * NX + pos), 2 * count)]

        def ref_b(pos, zpos, count):
            return gath[level].at[pl.ds(64 + 2 * (pos * NZ + zpos), 2 * count)]

        sib_sem = sem("sib")

        def share(first, count):
            put(
                gath[level].at[pl.ds(first, count)], gath[level].at[pl.ds(128 + first, count)],
                sib_sem, sib, g_sem,
            )

        def share_a(a, pos, count):
            share(2 * (a * NX + pos), 2 * count)

        def share_b(pos, zpos, count):
            share(64 + 2 * (pos * NZ + zpos), 2 * count)

        def z_a(a, p, direction):
            to = (a + direction) % NZ
            put(
                ref_a(a, 2 * p, 2), ref_a(to, 2 * p, 2), sem(("az", to, p)),
                z_up if direction == 1 else z_dn, g_sem,
            )

        def z_b(a, direction):
            to = (a + direction) % NZ
            put(
                ref_b(0, Z_POS[a], 1), ref_b(0, Z_POS[to], 1), sem(("bz", to)),
                z_up if direction == 1 else z_dn, g_sem,
            )

        def x_b(group):
            zpos, count = GROUPS[group]
            put(ref_b(0, zpos, count), ref_b(1, zpos, count), sem(("bl", group)), x_rt, g_sem)
            put(ref_b(0, zpos, count), ref_b(2, zpos, count), sem(("br", group)), x_lf, g_sem)

        def far_b(group):
            zpos, count = GROUPS[group]
            if group in (0, 1, 4):
                put(ref_b(1, zpos, count), ref_b(3, zpos, count), sem(("b2", group)), x_rt, g_sem)
            else:
                put(ref_b(2, zpos, count), ref_b(3, zpos, count), sem(("b2", group)), x_lf, g_sem)

        def got_x_b(group):
            zpos, count = GROUPS[group]
            if group in (0, 1, 4):
                take(ref_b(1, zpos, count), sem(("bl", group)))
                far_b(group)
                take(ref_b(2, zpos, count), sem(("br", group)))
            else:
                take(ref_b(2, zpos, count), sem(("br", group)))
                far_b(group)
                take(ref_b(1, zpos, count), sem(("bl", group)))
            share_b(1, zpos, count)
            share_b(2, zpos, count)

        def got_z_b(a):
            take(ref_b(0, Z_POS[a], 1), sem(("bz", a)))

        def got_z_a(a, p):
            take(ref_a(a, 2 * p, 2), sem(("az", a, p)))

        gath[level][pl.ds(0, 2)] = fwd[level, pl.ds(0, 2)]
        gath[level][pl.ds(64, 2)] = fwd[level, pl.ds(2, 2)]
        z_b(0, 1)
        z_b(0, -1)
        put(ref_a(0, 0, 1), ref_a(0, 1, 1), sem("ax1"), x_rt, g_sem)
        put(ref_a(0, 0, 1), ref_a(0, 2, 1), sem("ax3"), x_lf, g_sem)
        put(ref_a(0, 0, 1), ref_a(0, 3, 1), sem("ax2"), x_far, g_sem)
        x_b(0)
        share_a(0, 0, 1)
        share_b(0, 0, 1)
        between()
        take(ref_a(0, 1, 1), sem("ax1"))
        z_a(0, 0, 1)
        z_a(0, 0, -1)
        got_z_b(1)
        z_b(1, 1)
        got_z_b(7)
        z_b(7, -1)
        x_b(1)
        take(ref_a(0, 2, 1), sem("ax3"))
        take(ref_a(0, 3, 1), sem("ax2"))
        z_a(0, 1, 1)
        z_a(0, 1, -1)
        share_a(0, 1, 3)
        share_b(0, 1, 2)
        got_x_b(0)
        got_z_b(2)
        z_b(2, 1)
        got_z_b(6)
        z_b(6, -1)
        x_b(2)
        got_z_a(1, 0)
        z_a(1, 0, 1)
        got_z_a(7, 0)
        z_a(7, 0, -1)
        got_z_a(1, 1)
        z_a(1, 1, 1)
        got_z_a(7, 1)
        z_a(7, 1, -1)
        share_a(1, 0, 4)
        share_a(7, 0, 4)
        share_b(0, 3, 2)
        got_x_b(1)
        got_z_b(3)
        z_b(3, 1)
        got_z_b(5)
        x_b(3)
        got_z_a(2, 0)
        z_a(2, 0, 1)
        got_z_a(6, 0)
        z_a(6, 0, -1)
        got_z_a(2, 1)
        z_a(2, 1, 1)
        got_z_a(6, 1)
        z_a(6, 1, -1)
        share_a(2, 0, 4)
        share_a(6, 0, 4)
        share_b(0, 5, 2)
        got_x_b(2)
        got_z_b(4)
        x_b(4)
        share_b(0, 7, 1)
        got_x_b(3)
        got_z_a(3, 0)
        z_a(3, 0, 1)
        got_z_a(5, 1)
        z_a(5, 1, -1)
        got_z_a(3, 1)
        got_z_a(5, 0)
        share_a(3, 0, 4)
        share_a(5, 0, 4)
        got_x_b(4)
        for group in range(5):
            zpos, count = GROUPS[group]
            take(ref_b(3, zpos, count), sem(("b2", group)))
        share_b(3, 0, 8)
        got_z_a(4, 0)
        got_z_a(4, 1)
        share_a(4, 0, 4)
        take(gath[level].at[pl.ds(128, 128)], sib_sem)
        sent(252, g_sem)

    def reduce_row(low_level):
        r_sem = send_sem.at[0]
        ids = {}

        def sem(key):
            return rs_sem.at[low_level, ids.setdefault(key, len(ids))]

        def own_a(a, p):
            return own.at[low_level, pl.ds(2 * (a * NX + 2 * p), 4)]

        def own_b(pos, zpos, count):
            return own.at[low_level, pl.ds(64 + 2 * (pos * NZ + zpos), 2 * count)]

        def ref_az(a, p, direction):
            buffer, slot = (up_a, a) if direction == 1 else (dn_a, (NZ - a) % NZ)
            return buffer.at[low_level, slot, p]

        def send_az(src, a, p, direction):
            to = a - direction if direction == 1 else a + 1
            to = to % NZ
            put(
                src, ref_az(to, p, direction), sem(("az", to, p, direction)),
                z_up if direction == 1 else z_dn, r_sem,
            )

        def pass_az(a, p, direction):
            ref = ref_az(a, p, direction)
            take(ref, sem(("az", a, p, direction)))
            if a:
                ref[...] += own_a(a, p)[...]
                send_az(ref, a, p, direction)

        zs = [(7, 1), (3, 4), (0, 3)]

        def mid(buffer, part_no):
            zpos, count = zs[part_no]
            return buffer.at[low_level, pl.ds(2 * zpos, 2 * count)]

        put(own_b(3, 7, 1), mid(mid_l, 0), sem(("m", 0)), x_rt, r_sem)
        put(own_b(2, 7, 1), mid(fin_r, 0), sem(("fr", 0)), x_lf, r_sem)
        send_az(own_a(4, 0), 4, 0, 1)
        send_az(own_a(4, 1), 4, 1, -1)
        put(own_b(3, 3, 4), mid(mid_r, 1), sem(("m", 1)), x_lf, r_sem)
        put(own_b(3, 0, 3), mid(mid_l, 2), sem(("m", 2)), x_rt, r_sem)
        send_az(own_a(3, 1), 3, 1, 1)
        send_az(own_a(5, 0), 5, 0, -1)
        put(own_b(1, 3, 4), mid(fin_l, 1), sem(("fl", 1)), x_rt, r_sem)
        put(own_b(2, 0, 3), mid(fin_r, 2), sem(("fr", 2)), x_lf, r_sem)

        take(mid(mid_l, 0), sem(("m", 0)))
        mid(mid_l, 0)[...] += own_b(1, 7, 1)[...]
        put(mid(mid_l, 0), mid(fin_l, 0), sem(("fl", 0)), x_rt, r_sem)
        pass_az(3, 0, 1)
        pass_az(5, 1, -1)
        take(mid(mid_r, 1), sem(("m", 1)))
        mid(mid_r, 1)[...] += own_b(2, 3, 4)[...]
        put(mid(mid_r, 1), mid(fin_r, 1), sem(("fr", 1)), x_lf, r_sem)
        pass_az(2, 1, 1)
        pass_az(6, 0, -1)
        take(mid(mid_l, 2), sem(("m", 2)))
        mid(mid_l, 2)[...] += own_b(1, 0, 3)[...]
        put(mid(mid_l, 2), mid(fin_l, 2), sem(("fl", 2)), x_rt, r_sem)

        def ref_bz(a, direction):
            buffer, slot = (up_z, a) if direction == 1 else (dn_z, (NZ - a) % NZ)
            return buffer.at[low_level, slot]

        def send_bz(src, a, direction):
            to = (a - 1 if direction == 1 else a + 1) % NZ
            put(
                src, ref_bz(to, direction), sem(("bz", to, direction)),
                z_up if direction == 1 else z_dn, r_sem,
            )

        def pass_bz(a, direction):
            ref = ref_bz(a, direction)
            take(ref, sem(("bz", a, direction)))
            if a:
                ref[...] += col_z[low_level, pl.ds(2 * Z_POS[a], 2)]
                send_bz(ref, a, direction)

        def finish_x(part_no):
            zpos, count = zs[part_no]
            take(mid(fin_l, part_no), sem(("fl", part_no)))
            take(mid(fin_r, part_no), sem(("fr", part_no)))
            col_z[low_level, pl.ds(2 * zpos, 2 * count)] = (
                own_b(0, zpos, count)[...] + mid(fin_l, part_no)[...] + mid(fin_r, part_no)[...]
            )

        def col_at(a):
            return col_z.at[low_level, pl.ds(2 * Z_POS[a], 2)]

        finish_x(0)
        send_bz(col_at(4), 4, 1)
        pass_az(2, 0, 1)
        pass_az(6, 1, -1)
        finish_x(1)
        send_bz(col_at(5), 5, -1)
        pass_bz(3, 1)
        pass_az(1, 1, 1)
        pass_az(7, 0, -1)
        pass_bz(6, -1)
        pass_bz(2, 1)
        finish_x(2)
        pass_az(1, 0, 1)
        pass_az(7, 1, -1)
        pass_bz(7, -1)
        pass_bz(1, 1)
        for p in (1, 0):
            pass_az(0, p, 1)
            pass_az(0, p, -1)
            row_x[low_level, p] = own_a(0, p)[...] + up_a[low_level, 0, p] + dn_a[low_level, 0, p]
            if p == 1:
                put(row_x.at[low_level, 1, pl.ds(2, 2)], in_x.at[low_level, 2], sem("x3"), x_far, r_sem)
                put(row_x.at[low_level, 1, pl.ds(0, 2)], in_x.at[low_level, 1], sem("x2"), x_lf, r_sem)
            else:
                put(row_x.at[low_level, 0, pl.ds(2, 2)], in_x.at[low_level, 0], sem("x1"), x_rt, r_sem)
        pass_bz(0, -1)
        pass_bz(0, 1)
        half_b = col_z[low_level, pl.ds(0, 2)] + up_z[low_level, 0] + dn_z[low_level, 0]
        for slot in (2, 1, 0):
            take(in_x.at[low_level, slot], sem("x%d" % (slot + 1)))
        half_a = (
            row_x[low_level, 0, pl.ds(0, 2)] + in_x[low_level, 0] + in_x[low_level, 1] + in_x[low_level, 2]
        )
        sent(188, r_sem)
        return half_a, half_b

    for level in (1, 2, 3, 0):
        for t in (1, 2, 3):
            ref = inv.at[level, :, c]
            put(ref, ref, inv_sem.at[level, t - 1], col_dev[t], send_sem.at[1])

    def whole_inv(level):
        for t in (1, 2, 3):
            take(inv.at[level, :, 0], inv_sem.at[level, t - 1])

    def forward_level(low_level):
        level = low_level + 1

        def between():
            if low_level == 0:
                loads[2].wait()
                loads[3].wait()

            for j in range(4):
                own_part[j] = exact_dot(inv[level, j, c], rhs[level, j])
            for j in range(4):
                low_t[j] = low[low_level, j].T

        gather_row(low_level, between)
        whole_inv(level)
        for j in range(4):
            picked = jnp.concatenate([gath[low_level][fwd_idx[low_level, 16 * j + d]] for d in range(16)], axis=0)
            update = exact_dot(low_t[j], picked)
            done = exact_dot(inv[level, j].reshape(128, 128), update)
            for piece in range(4):
                part[low_level, piece, j] = done[32 * piece : 32 * piece + 32]
        for t in (1, 2, 3):
            put(
                part.at[low_level, (c + t) % 4], col_in.at[low_level, t - 1],
                col_sem.at[low_level, t - 1], col_dev[t], send_sem.at[0],
            )
        for t in (1, 2, 3):
            take(col_in.at[low_level, t - 1], col_sem.at[low_level, t - 1])
        fwd[level] = (
            own_part[...] - part[low_level, c]
            - col_in[low_level, 0] - col_in[low_level, 1] - col_in[low_level, 2]
        )
        sent(12, send_sem.at[0])

    for low_level in range(3):
        forward_level(low_level)
    whole_inv(0)

    def solve_level(level):
        ref = rest.at[level, c]
        for t in (1, 2, 3):
            put(ref, ref, col_sem.at[3 + level, t - 1], col_dev[t], send_sem.at[0])
        for t in (1, 2, 3):
            take(ref, col_sem.at[3 + level, t - 1])
        for j in range(4):
            whole = inv[level, j].reshape(128, 128)
            sol[j] = exact_dot(whole.T, rest[level, :, j].reshape(128, 128))
        for j in range(4):
            out_ref[level, j] = sol[j, pl.ds(pl.multiple_of(32 * c, 32), 32), :]
        sent(12, send_sem.at[0])

    rest[3, c] = fwd[3]

    def backward_level(low_level):
        solve_level(low_level + 1)
        t_sem = rs_sem.at[low_level, 63]
        for j in range(4):
            product = exact_dot(low[low_level, j], sol[j])
            terms[low_level][pl.ds(16 * j, 16)] = product.reshape(16, 32, 128)
            put(
                terms[low_level].at[pl.ds(16 * j, 16)], terms[low_level].at[pl.ds(64 + 16 * j, 16)],
                t_sem, sib, send_sem.at[0],
            )
        take(terms[low_level].at[pl.ds(64, 64)], t_sem)

        def build(place, inner):
            own[low_level, place] = (
                terms[low_level][bwd_idx[low_level, 4 * place]]
                + terms[low_level][bwd_idx[low_level, 4 * place + 1]]
                + terms[low_level][bwd_idx[low_level, 4 * place + 2]]
                + terms[low_level][bwd_idx[low_level, 4 * place + 3]]
            )
            return inner

        lax.fori_loop(0, 128, build, 0)
        half_a, half_b = reduce_row(low_level)
        rest[low_level, c, pl.ds(0, 2)] = fwd[low_level, pl.ds(0, 2)] - half_a
        rest[low_level, c, pl.ds(2, 2)] = fwd[low_level, pl.ds(2, 2)] - half_b

    for low_level in (2, 1, 0):
        backward_level(low_level)
    solve_level(0)
    sent(48, send_sem.at[1])


def on_device(right_sides, inverse_diag, lower_blocks, depends_on):
    row = lax.axis_index("row")
    z, x, core = row // (2 * NX), row // 2 % NX, row % 2
    mine = lax.dynamic_slice(depends_on, (0, 4 * row, 0), (3, 4, 16)).reshape(3, 64)
    other = lax.dynamic_slice(depends_on, (0, 4 * (row + 1 - 2 * core), 0), (3, 4, 16)).reshape(3, 64)
    place, owner_core = block_place(mine, lambda zz: z - zz, lambda xx: x - xx)
    fwd_idx = place + jnp.where(owner_core == core, 0, 128)
    lists = []
    for base, wanted in ((0, mine), (64, other)):
        place, owner_core = block_place(wanted, lambda zz: zz - z, lambda xx: xx - x)
        place = jnp.where(owner_core == core, place, -1)
        match = place[:, None, :] == jnp.arange(128, dtype=jnp.int32)[None, :, None]
        entry = jnp.arange(64, dtype=jnp.int32)[None, None, :]
        first = jnp.min(jnp.where(match, entry, 64), axis=2)
        last = jnp.max(jnp.where(match, entry, -1), axis=2)
        lists.append(jnp.where(first == 64, 128, base + first))
        lists.append(jnp.where(last > first, base + last, 128))
    bwd_idx = jnp.stack(lists, axis=2).reshape(3, 512)

    f32 = jnp.float32

    def vmem(*shape):
        return pltpu.VMEM(shape, f32)

    any_spec = pl.BlockSpec(memory_space=pl.ANY)
    smem_spec = pl.BlockSpec(memory_space=pltpu.SMEM)
    block = (32, 128)
    return pl.pallas_call(
        kernel,
        out_shape=jax.ShapeDtypeStruct((4, 4, 32, 128), f32),
        in_specs=[smem_spec, smem_spec, any_spec, any_spec, any_spec],
        out_specs=pl.BlockSpec(memory_space=pltpu.VMEM),
        scratch_shapes=[
            vmem(4, 4, 128, 128),
            vmem(4, 4, 4, *block),
            vmem(3, 4, 512, 128),
            vmem(4, 128, 512),
            vmem(4, 4, *block),
            vmem(4, *block),
            vmem(256, *block),
            vmem(256, *block),
            vmem(256, *block),
            vmem(3, 4, 4, *block),
            vmem(3, 3, 4, *block),
            vmem(4, 4, 4, *block),
            vmem(4, 128, 128),
            vmem(129, *block),
            vmem(129, *block),
            vmem(129, *block),
            vmem(3, 128, *block),
            vmem(3, 4, 2, 4, *block),
            vmem(3, 4, 2, 4, *block),
            vmem(3, 2, 4, *block),
            vmem(3, 3, 2, *block),
            vmem(3, 16, *block),
            vmem(3, 16, *block),
            vmem(3, 16, *block),
            vmem(3, 16, *block),
            vmem(3, 16, *block),
            vmem(3, 4, 2, *block),
            vmem(3, 4, 2, *block),
            pltpu.SemaphoreType.DMA((4,)),
            pltpu.SemaphoreType.DMA((2,)),
            pltpu.SemaphoreType.DMA((4, 3)),
            pltpu.SemaphoreType.DMA((3, 64)),
            pltpu.SemaphoreType.DMA((3, 64)),
            pltpu.SemaphoreType.DMA((7, 3)),
        ],
        compiler_params=pltpu.CompilerParams(
            collective_id=0, has_side_effects=True, vmem_limit_bytes=60 * 1024 * 1024
        ),
    )(fwd_idx, bwd_idx, right_sides, inverse_diag, lower_blocks.reshape(3, 4, 512, 128))


def solution(mesh):
    return jax.shard_map(
        on_device,
        mesh=mesh,
        in_specs=(
            P(None, "row", None, None),
            P(None, "row", "col", None),
            P(None, "row", None, "col", None),
            P(),
        ),
        out_specs=P(None, "row", "col", None),
        check_vma=False,
    )
```

time: 1090 us -> 212 us (0.19)
  waiting for transfers between devices: 983 us -> 0 us
  Pallas kernels: 0 us -> 207 us
  matrix products: 57.1 us -> 0 us
  local copies, waits for them, and re-layouts: 22.8 us -> 3.8 us
  between operations: 13.7 us -> 0.06 us
    reduce_scatter x3 -> x0, waiting for transfers between devices: 431 us -> none  [return_terms(): lax.psum_scatter(jnp.einsum('me,erk->mrk', owners, terms, precision=exact...]
    psum x7 -> x0, waiting for transfers between devices: 318 us -> none  [the longest x4 184 us: backward_solve(): return lax.psum(partial_value, 'col')]
    all_gather x3 -> x0, waiting for transfers between devices: 235 us -> none  [fetch_blocks(): shard_rows = lax.all_gather(previous, 'row', axis=0, tiled=True)]
    pallas_call x0 -> x1, Pallas kernels: none -> 207 us  [on_device(): pl.pallas_call(kernel, out_shape=jax.ShapeDtypeStruct((4, 4, 32, 128), f3...]
    dot_general x20 -> x0, matrix products: 57.1 us -> none  [the longest x3 18.4 us: fetch_blocks(): return jnp.einsum('en,nrk->erk', chooser, shard_rows, precision=exact_mode)]
    dot_general x3 -> x0, local copies, waits for them, and re-layouts: 13.1 us -> none  [return_terms(): jnp.einsum('me,erk->mrk', owners, terms, precision=exact_mode)]
  transfers between devices with their start and end apart: 13 -> 0, of which waited for: 13 -> 0; matrix products, arithmetic and copies ran while one was open for 1% -> 0% of each run, Pallas kernels for 0% -> 0%
where the time goes in v1:
time: 212 us
  Pallas kernels  207 us (98%)
  local copies, waits for them, and re-layouts  3.8 us (2%)
    pallas_call x1, Pallas kernels, on_device(): pl.pallas_call(kernel, out_shape=jax.ShapeDtypeStruct((4, 4, 32, 128), f3...  207 us

profile of v1, /device:TPU:2, one launch (start us, length us, event | category | flops | bytes accessed | tf_op | source)
XLA Modules:
  0.0 212.0 jit_solution(5091587777987777861)
XLA Ops:
  0.0 0.9 constant_dynamic-slice_fusion
  0.9 0.1 copy.12
  1.0 0.1 reshape.394
  1.1 0.1 copy.11
  1.2 0.1 reshape.393
  1.2 0.1 add_select_fusion.20
  1.3 0.6 select_add_fusion.fwd_idx
  1.9 0.1 select_reduce_fusion.3
  2.1 0.1 select_reduce_fusion.1
  2.2 0.1 copy.13
  2.3 0.8 reshape.395.bwd_idx
  3.1 207.2 %shard_map.46 = f32[4,4,32,128]{3,2,1,0:T(8,128)} custom-call(s32[3,64]{1,0:T(4,128)} %select_add_fusion.fwd_idx, s32[3,512]{1,0:T(4,128)} %reshape.395.bwd_idx, f32[4,4,128,128]{3,2,1,0:T(8,128)} %rhs_hbm.1, f32[4,4,32,128]{3,2,1,0:T(8,128)} %inv_hbm.1, f32[3,4,512,128]{3,2,1,0:T(8,128)} %bitcast.10), custom_call_target="tpu_custom_call" | custom-call | tf_op jit(solution)/shard_map/pallas_call | solution.py:497
  210.3 1.7 copy.15
  (3 shorter events, 0.0 us)

commit v2 on v1

v2 whole, which is shorter than its diff:
```python
import jax
import jax.numpy as jnp
from jax import lax
from jax.experimental import pallas as pl
from jax.experimental.pallas import tpu as pltpu
from jax.sharding import PartitionSpec as P

MESH = pl.DeviceIdType.MESH
NZ, NX = 8, 4
X_POS = {0: 0, 1: 1, 3: 2, 2: 3}
Z_POS = {0: 0, 1: 1, 7: 2, 2: 3, 6: 4, 3: 5, 5: 6, 4: 7}
GROUPS = [(0, 1), (1, 2), (3, 2), (5, 2), (7, 1)]


def split(v):
    high = v.astype(jnp.bfloat16)
    return high, (v - high.astype(jnp.float32)).astype(jnp.bfloat16)


def split_dot(a, b):
    def dot(u, v):
        return jnp.dot(u, v, preferred_element_type=jnp.float32)

    return dot(a[0], b[0]) + (dot(a[0], b[1]) + dot(a[1], b[0]))


def exact_dot(a, b):
    return split_dot(split(a), split(b))


def ring_pos(distance, size):
    return jnp.where(
        distance == 0,
        0,
        jnp.where(distance <= size // 2, 2 * distance - 1, 2 * (size - distance)),
    )


def block_place(block, z_of, x_of):
    owner, local = block // 4, block % 4
    a = z_of(owner // (2 * NX)) % NZ
    b = x_of(owner // 2 % NX) % NX
    slot_a = a * NX + ring_pos(b, NX)
    slot_b = ring_pos(b, NX) * NZ + ring_pos(a, NZ)
    return jnp.where(local < 2, 2 * slot_a, 64 + 2 * slot_b) + local % 2, owner % 2


def kernel(
    fwd_idx, bwd_idx, rhs_hbm, inv_hbm, low_hbm, out_ref,
    rhs, inv, low, low_hi, low_lo, fwd, own_part, gath_0, gath_1, gath_2, part, col_in, rest,
    sol, terms_0, terms_1, terms_2, others_0, others_1, others_2, own, up_a, dn_a, row_x, in_x, mid_l, mid_r, fin_l, fin_r, col_z, in_z,
    load_sem, send_sem, inv_sem, ag_sem, rs_sem, col_sem,
):
    gath, terms = (gath_0, gath_1, gath_2), (terms_0, terms_1, terms_2)
    others = (others_0, others_1, others_2)
    row, c = lax.axis_index("row"), lax.axis_index("col")
    z, x, core = row // (2 * NX), row // 2 % NX, row % 2

    def at_row(zz, xx, cc):
        return ((zz * NX + xx) * 2 + cc, c)

    z_dev = [None] + [at_row((z + a) % NZ, x, core) for a in range(1, NZ)]
    x_rt, x_lf = at_row(z, (x + 1) % NX, core), at_row(z, (x + NX - 1) % NX, core)
    x_far = at_row(z, (x + 2) % NX, core)
    sib = at_row(z, x, 1 - core)
    col_dev = [None] + [(row, (c + t) % 4) for t in (1, 2, 3)]

    loads = [
        pltpu.make_async_copy(inv_hbm, inv.at[:, :, c], load_sem.at[0]),
        pltpu.make_async_copy(rhs_hbm.at[0], rhs.at[0], load_sem.at[1]),
        pltpu.make_async_copy(rhs_hbm.at[pl.ds(1, 3)], rhs.at[pl.ds(1, 3)], load_sem.at[2]),
        pltpu.make_async_copy(low_hbm, low, load_sem.at[3]),
    ]
    for load in loads:
        load.start()

    barrier = pltpu.get_barrier_semaphore()
    partners = [z_dev[a] for a in (1, 2, 6, 7)] + [x_rt, x_lf, x_far, sib] + col_dev[1:]
    for partner in partners:
        pl.semaphore_signal(barrier, inc=1, device_id=partner, device_id_type=MESH)

    for level in range(3):
        terms[level][64] = jnp.zeros((32, 128), jnp.float32)
        others[level][64] = jnp.zeros((32, 128), jnp.float32)
    loads[0].wait()
    loads[1].wait()
    for j in range(4):
        fwd[0, j] = exact_dot(inv[0, j, c], rhs[0, j])
    pl.semaphore_wait(barrier, len(partners))

    def put(src, dst, sem, device, out_sem):
        pltpu.make_async_remote_copy(
            src_ref=src, dst_ref=dst, send_sem=out_sem, recv_sem=sem, device_id=device, device_id_type=MESH
        ).start()

    def take(dst, sem, device=None):
        pltpu.make_async_remote_copy(
            src_ref=dst, dst_ref=dst, send_sem=send_sem.at[0], recv_sem=sem, device_id=sib, device_id_type=MESH
        ).wait_recv()

    def sent(count, out_sem):
        ref = gath[0].at[pl.ds(0, count)]
        pltpu.make_async_remote_copy(
            src_ref=ref, dst_ref=ref, send_sem=out_sem, recv_sem=out_sem, device_id=sib, device_id_type=MESH
        ).wait_send()

    def gather_row(level, ready, between):
        g_sem = send_sem.at[0]
        ids = {}

        def sem(key):
            return ag_sem.at[level, ids.setdefault(key, len(ids))]

        def ref_a(a, pos, count):
            return gath[level].at[pl.ds(2 * (a * NX + pos), 2 * count)]

        def ref_b(pos, zpos, count):
            return gath[level].at[pl.ds(64 + 2 * (pos * NZ + zpos), 2 * count)]

        sib_sem = sem("sib")

        def share(first, count):
            put(
                gath[level].at[pl.ds(first, count)], gath[level].at[pl.ds(128 + first, count)],
                sib_sem, sib, g_sem,
            )

        def share_a(a, pos, count):
            share(2 * (a * NX + pos), 2 * count)

        def share_b(pos, zpos, count):
            share(64 + 2 * (pos * NZ + zpos), 2 * count)

        def z_a(a, p, direction, hops=1):
            to = (a + direction * hops) % NZ
            put(ref_a(a, 2 * p, 2), ref_a(to, 2 * p, 2), sem(("az", to, p)), z_dev[direction * hops % NZ], g_sem)

        def x_b(group):
            zpos, count = GROUPS[group]
            put(ref_b(0, zpos, count), ref_b(1, zpos, count), sem(("bl", group)), x_rt, g_sem)
            put(ref_b(0, zpos, count), ref_b(2, zpos, count), sem(("br", group)), x_lf, g_sem)

        def far_b(group):
            zpos, count = GROUPS[group]
            if group in (0, 1, 4):
                put(ref_b(1, zpos, count), ref_b(3, zpos, count), sem(("b2", group)), x_rt, g_sem)
            else:
                put(ref_b(2, zpos, count), ref_b(3, zpos, count), sem(("b2", group)), x_lf, g_sem)

        def got_x_b(group):
            zpos, count = GROUPS[group]
            if group in (0, 1, 4):
                take(ref_b(1, zpos, count), sem(("bl", group)))
                far_b(group)
                take(ref_b(2, zpos, count), sem(("br", group)))
            else:
                take(ref_b(2, zpos, count), sem(("br", group)))
                far_b(group)
                take(ref_b(1, zpos, count), sem(("bl", group)))
            share_b(1, zpos, count)
            share_b(2, zpos, count)

        def got_far_b(group):
            zpos, count = GROUPS[group]
            take(ref_b(3, zpos, count), sem(("b2", group)))
            share_b(3, zpos, count)

        def z_b(a, hops):
            to = (a + hops) % NZ
            put(ref_b(0, Z_POS[a], 1), ref_b(0, Z_POS[to], 1), sem(("bz", to)), z_dev[hops % NZ], g_sem)

        def got_z_b(a):
            take(ref_b(0, Z_POS[a], 1), sem(("bz", a)))
            if a == 2:
                z_b(2, 2)
                z_b(2, 1)
            elif a == 6:
                z_b(6, -1)

        def got_z_a(a, p):
            take(ref_a(a, 2 * p, 2), sem(("az", a, p)))

        ready(level, 0)
        gath[level][pl.ds(0, 2)] = fwd[level, pl.ds(0, 2)]
        put(ref_a(0, 0, 1), ref_a(0, 1, 1), sem("ax1"), x_rt, g_sem)
        put(ref_a(0, 0, 1), ref_a(0, 3, 1), sem("ax2"), x_far, g_sem)
        put(ref_a(0, 0, 1), ref_a(0, 2, 1), sem("ax3"), x_lf, g_sem)
        share_a(0, 0, 1)
        ready(level, 1)
        gath[level][pl.ds(64, 2)] = fwd[level, pl.ds(2, 2)]
        for hops in (2, -2, 1, -1):
            z_b(0, hops)
        x_b(0)
        share_b(0, 0, 1)
        between()
        take(ref_a(0, 1, 1), sem("ax1"))
        z_a(0, 0, 1)
        z_a(0, 0, -1)
        take(ref_a(0, 2, 1), sem("ax3"))
        take(ref_a(0, 3, 1), sem("ax2"))
        z_a(0, 1, 1)
        z_a(0, 1, -1)
        share_a(0, 1, 3)
        for group, pair in ((1, (1, 7)), (2, (2, 6))):
            for a in pair:
                got_z_b(a)
            x_b(group)
            share_b(0, *GROUPS[group])
        got_x_b(0)
        for p in (0, 1):
            got_z_a(1, p)
            z_a(1, p, 1)
            got_z_a(7, p)
            z_a(7, p, -1)
        share_a(1, 0, 4)
        share_a(7, 0, 4)
        got_z_b(3)
        got_z_b(5)
        x_b(3)
        share_b(0, *GROUPS[3])
        got_x_b(1)
        got_far_b(0)
        got_z_b(4)
        x_b(4)
        share_b(0, *GROUPS[4])
        got_x_b(2)
        got_z_a(2, 0)
        z_a(2, 0, 1, 2)
        z_a(2, 0, 1)
        got_z_a(6, 0)
        z_a(6, 0, -1)
        got_z_a(6, 1)
        z_a(6, 1, -1, 2)
        z_a(6, 1, -1)
        got_z_a(2, 1)
        z_a(2, 1, 1)
        share_a(2, 0, 4)
        share_a(6, 0, 4)
        got_far_b(1)
        got_x_b(3)
        got_x_b(4)
        got_far_b(2)
        for a in (3, 5):
            got_z_a(a, 0)
            got_z_a(a, 1)
            share_a(a, 0, 4)
        got_far_b(3)
        got_far_b(4)
        got_z_a(4, 0)
        got_z_a(4, 1)
        share_a(4, 0, 4)
        take(gath[level].at[pl.ds(128, 128)], sib_sem)
        sent(252, g_sem)

    def reduce_row(low_level, build):
        r_sem = send_sem.at[0]
        ids = {}

        def sem(key):
            return rs_sem.at[low_level, ids.setdefault(key, len(ids))]

        def own_a(a, p):
            return own.at[low_level, pl.ds(2 * (a * NX + 2 * p), 4)]

        def own_b(pos, zpos, count):
            return own.at[low_level, pl.ds(64 + 2 * (pos * NZ + zpos), 2 * count)]

        def ref_az(hops, p, direction):
            return (up_a if direction == 1 else dn_a).at[low_level, hops, p]

        def send_az(src, hops, p, direction, step=1):
            slot = hops - step if step == 1 else 3
            put(src, ref_az(slot, p, direction), sem(("az", slot, p, direction)), z_dev[direction * step % NZ], r_sem)

        def pass_az(hops, p, direction):
            ref = ref_az(hops, p, direction)
            take(ref, sem(("az", hops, p, direction)))
            if hops == 2 and p == (0 if direction == 1 else 1):
                far = ref_az(3, p, direction)
                take(far, sem(("az", 3, p, direction)))
                ref[...] += own_a(direction * hops % NZ, p)[...] + far[...]
                send_az(ref, hops, p, direction)
            elif hops:
                ref[...] += own_a(direction * hops % NZ, p)[...]
                send_az(ref, hops, p, direction)

        zs = [(7, 1), (3, 4), (0, 3)]

        def mid(buffer, part_no):
            zpos, count = zs[part_no]
            return buffer.at[low_level, pl.ds(2 * zpos, 2 * count)]

        build(112, 16)
        put(own_b(3, 7, 1), mid(mid_l, 0), sem(("m", 0)), x_rt, r_sem)
        put(own_b(3, 3, 4), mid(mid_r, 1), sem(("m", 1)), x_lf, r_sem)
        put(own_b(3, 0, 3), mid(mid_l, 2), sem(("m", 2)), x_rt, r_sem)
        build(24, 24)
        send_az(own_a(4, 0), 4, 0, 1, 2)
        send_az(own_a(4, 1), 4, 1, -1, 2)
        send_az(own_a(3, 0), 3, 0, 1)
        send_az(own_a(5, 1), 3, 1, -1)
        send_az(own_a(3, 1), 3, 1, 1)
        send_az(own_a(5, 0), 3, 0, -1)
        build(80, 32)
        put(own_b(2, 7, 1), mid(fin_r, 0), sem(("fr", 0)), x_lf, r_sem)
        put(own_b(1, 3, 4), mid(fin_l, 1), sem(("fl", 1)), x_rt, r_sem)
        put(own_b(2, 0, 3), mid(fin_r, 2), sem(("fr", 2)), x_lf, r_sem)
        build(0, 24)
        build(48, 32)

        take(mid(mid_l, 0), sem(("m", 0)))
        mid(mid_l, 0)[...] += own_b(1, 7, 1)[...]
        put(mid(mid_l, 0), mid(fin_l, 0), sem(("fl", 0)), x_rt, r_sem)
        take(mid(mid_r, 1), sem(("m", 1)))
        mid(mid_r, 1)[...] += own_b(2, 3, 4)[...]
        put(mid(mid_r, 1), mid(fin_r, 1), sem(("fr", 1)), x_lf, r_sem)
        pass_az(2, 1, 1)
        pass_az(2, 0, -1)
        take(mid(mid_l, 2), sem(("m", 2)))
        mid(mid_l, 2)[...] += own_b(1, 0, 3)[...]
        put(mid(mid_l, 2), mid(fin_l, 2), sem(("fl", 2)), x_rt, r_sem)
        pass_az(2, 0, 1)
        pass_az(2, 1, -1)

        def finish_x(part_no):
            zpos, count = zs[part_no]
            take(mid(fin_l, part_no), sem(("fl", part_no)))
            take(mid(fin_r, part_no), sem(("fr", part_no)))
            col_z[low_level, pl.ds(2 * zpos, 2 * count)] = (
                own_b(0, zpos, count)[...] + mid(fin_l, part_no)[...] + mid(fin_r, part_no)[...]
            )

        def z_part(a):
            return col_z.at[low_level, pl.ds(2 * Z_POS[a], 2)]

        def send_bz(src, key, hops):
            put(src, in_z.at[low_level, key], sem(("bz", key)), z_dev[hops % NZ], r_sem)

        def got_bz(key):
            take(in_z.at[low_level, key], sem(("bz", key)))
            return in_z[low_level, key]

        finish_x(0)
        send_bz(z_part(4), 0, 2)
        pass_az(1, 1, 1)
        pass_az(1, 0, -1)
        finish_x(1)
        send_bz(z_part(3), 1, 1)
        send_bz(z_part(5), 2, -1)
        pass_az(1, 0, 1)
        pass_az(1, 1, -1)
        finish_x(2)
        send_bz(z_part(1), 5, 1)
        send_bz(z_part(7), 6, -1)
        z_part(2)[...] += got_bz(0) + got_bz(1)
        send_bz(z_part(2), 3, 2)
        z_part(6)[...] += got_bz(2)
        send_bz(z_part(6), 4, -2)
        for p in (1, 0):
            pass_az(0, p, 1)
            pass_az(0, p, -1)
            row_x[low_level, p] = own_a(0, p)[...] + up_a[low_level, 0, p] + dn_a[low_level, 0, p]
            if p == 1:
                put(row_x.at[low_level, 1, pl.ds(2, 2)], in_x.at[low_level, 2], sem("x3"), x_far, r_sem)
                put(row_x.at[low_level, 1, pl.ds(0, 2)], in_x.at[low_level, 1], sem("x2"), x_lf, r_sem)
            else:
                put(row_x.at[low_level, 0, pl.ds(2, 2)], in_x.at[low_level, 0], sem("x1"), x_rt, r_sem)
        half_b = col_z[low_level, pl.ds(0, 2)]
        for key in (5, 6, 3, 4):
            half_b = half_b + got_bz(key)
        start_solve(low_level, 1, fwd[low_level, pl.ds(2, 2)] - half_b)
        for slot in (2, 1, 0):
            take(in_x.at[low_level, slot], sem("x%d" % (slot + 1)))
        half_a = (
            row_x[low_level, 0, pl.ds(0, 2)] + in_x[low_level, 0] + in_x[low_level, 1] + in_x[low_level, 2]
        )
        start_solve(low_level, 0, fwd[low_level, pl.ds(0, 2)] - half_a)
        sent(188, r_sem)

    for level in (1, 2, 3, 0):
        for t in (1, 2, 3):
            ref = inv.at[level, :, c]
            put(ref, ref, inv_sem.at[level, t - 1], col_dev[t], send_sem.at[1])

    def whole_inv(level):
        for t in (1, 2, 3):
            take(inv.at[level, :, 0], inv_sem.at[level, t - 1])

    def forward_level(low_level):
        level = low_level + 1

        def between():
            if low_level == 0:
                loads[2].wait()
                loads[3].wait()

            for j in range(4):
                own_part[j] = exact_dot(inv[level, j, c], rhs[level, j])
            for j in range(4):
                low_hi[j], low_lo[j] = split(low[low_level, j].T)

        gather_row(low_level, finish_forward, between)
        whole_inv(level)
        for half in (0, 1):
            for j in (2 * half, 2 * half + 1):
                picked = jnp.concatenate(
                    [gath[low_level][fwd_idx[low_level, 16 * j + d]] for d in range(16)], axis=0
                )
                update = split_dot((low_hi[j], low_lo[j]), split(picked))
                done = exact_dot(inv[level, j].reshape(128, 128), update)
                for piece in range(4):
                    part[low_level, piece, j] = done[32 * piece : 32 * piece + 32]
            for t in (2, 1, 3):
                put(
                    part.at[low_level, (c + t) % 4, pl.ds(2 * half, 2)],
                    col_in.at[low_level, t - 1, pl.ds(2 * half, 2)],
                    col_sem.at[low_level, half, t - 1], col_dev[t], send_sem.at[2],
                )

    def finish_forward(level, half):
        if level == 0:
            return
        blocks = pl.ds(2 * half, 2)
        total = own_part[blocks] - part[level - 1, c, blocks]
        for t in (1, 3, 2):
            take(col_in.at[level - 1, t - 1, blocks], col_sem.at[level - 1, half, t - 1])
            total = total - col_in[level - 1, t - 1, blocks]
        fwd[level, blocks] = total

    for low_level in range(3):
        forward_level(low_level)
    whole_inv(0)

    def start_solve(level, half, value):
        blocks = pl.ds(2 * half, 2)
        rest[level, c, blocks] = value
        ref = rest.at[level, c, blocks]
        for t in (2, 1, 3):
            put(ref, ref, col_sem.at[3 + level, half, t - 1], col_dev[t], send_sem.at[2])

    def finish_solve(level, half, product):
        blocks = pl.ds(2 * half, 2)
        for t in (1, 3, 2):
            take(rest.at[level, c, blocks], col_sem.at[3 + level, half, t - 1])
        for j in (2 * half, 2 * half + 1):
            whole = inv[level, j].reshape(128, 128)
            sol[j] = exact_dot(whole.T, rest[level, :, j].reshape(128, 128))
            product(j)
            out_ref[level, j] = sol[j, pl.ds(pl.multiple_of(32 * c, 32), 32), :]

    for half in (1, 0):
        finish_forward(3, half)
        start_solve(3, half, fwd[3, pl.ds(2 * half, 2)])

    def backward_level(low_level):
        t_sem = rs_sem.at[low_level, 63]

        def product(j):
            value = exact_dot(low[low_level, j], sol[j])
            terms[low_level][pl.ds(16 * j, 16)] = value.reshape(16, 32, 128)
            put(
                terms[low_level].at[pl.ds(16 * j, 16)], others[low_level].at[pl.ds(16 * j, 16)],
                t_sem, sib, send_sem.at[0],
            )

        finish_solve(low_level + 1, 1, product)
        finish_solve(low_level + 1, 0, product)

        def build_mine(place, inner):
            own[low_level, place] = (
                terms[low_level][bwd_idx[low_level, 4 * place]]
                + terms[low_level][bwd_idx[low_level, 4 * place + 1]]
            )
            return inner

        def build_other(place, inner):
            own[low_level, place] += (
                others[low_level][bwd_idx[low_level, 4 * place + 2]]
                + others[low_level][bwd_idx[low_level, 4 * place + 3]]
            )
            return inner

        lax.fori_loop(0, 128, build_mine, 0, unroll=8)
        take(others[low_level].at[pl.ds(0, 64)], t_sem)

        def build(first, count):
            lax.fori_loop(first, first + count, build_other, 0, unroll=8)

        reduce_row(low_level, build)

    for low_level in (2, 1, 0):
        backward_level(low_level)
    for half in (1, 0):
        finish_solve(0, half, lambda j: None)
    sent(48, send_sem.at[1])
    sent(84, send_sem.at[2])


def on_device(right_sides, inverse_diag, lower_blocks, depends_on):
    row = lax.axis_index("row")
    z, x, core = row // (2 * NX), row // 2 % NX, row % 2
    mine = lax.dynamic_slice(depends_on, (0, 4 * row, 0), (3, 4, 16)).reshape(3, 64)
    other = lax.dynamic_slice(depends_on, (0, 4 * (row + 1 - 2 * core), 0), (3, 4, 16)).reshape(3, 64)
    place, owner_core = block_place(mine, lambda zz: z - zz, lambda xx: x - xx)
    fwd_idx = place + jnp.where(owner_core == core, 0, 128)
    lists = []
    for wanted in (mine, other):
        place, owner_core = block_place(wanted, lambda zz: zz - z, lambda xx: xx - x)
        place = jnp.where(owner_core == core, place, -1)
        match = place[:, None, :] == jnp.arange(128, dtype=jnp.int32)[None, :, None]
        entry = jnp.arange(64, dtype=jnp.int32)[None, None, :]
        first = jnp.min(jnp.where(match, entry, 64), axis=2)
        last = jnp.max(jnp.where(match, entry, -1), axis=2)
        lists.append(first)
        lists.append(jnp.where(last > first, last, 64))
    bwd_idx = jnp.stack(lists, axis=2).reshape(3, 512)

    f32 = jnp.float32

    def vmem(*shape):
        return pltpu.VMEM(shape, f32)

    any_spec = pl.BlockSpec(memory_space=pl.ANY)
    smem_spec = pl.BlockSpec(memory_space=pltpu.SMEM)
    block = (32, 128)
    return pl.pallas_call(
        kernel,
        out_shape=jax.ShapeDtypeStruct((4, 4, 32, 128), f32),
        in_specs=[smem_spec, smem_spec, any_spec, any_spec, any_spec],
        out_specs=pl.BlockSpec(memory_space=pltpu.VMEM),
        scratch_shapes=[
            vmem(4, 4, 128, 128),
            vmem(4, 4, 4, *block),
            vmem(3, 4, 512, 128),
            pltpu.VMEM((4, 128, 512), jnp.bfloat16),
            pltpu.VMEM((4, 128, 512), jnp.bfloat16),
            vmem(4, 4, *block),
            vmem(4, *block),
            vmem(256, *block),
            vmem(256, *block),
            vmem(256, *block),
            vmem(3, 4, 4, *block),
            vmem(3, 3, 4, *block),
            vmem(4, 4, 4, *block),
            vmem(4, 128, 128),
            vmem(65, *block),
            vmem(65, *block),
            vmem(65, *block),
            vmem(65, *block),
            vmem(65, *block),
            vmem(65, *block),
            vmem(3, 128, *block),
            vmem(3, 4, 2, 4, *block),
            vmem(3, 4, 2, 4, *block),
            vmem(3, 2, 4, *block),
            vmem(3, 3, 2, *block),
            vmem(3, 16, *block),
            vmem(3, 16, *block),
            vmem(3, 16, *block),
            vmem(3, 16, *block),
            vmem(3, 16, *block),
            vmem(3, 7, 2, *block),
            pltpu.SemaphoreType.DMA((4,)),
            pltpu.SemaphoreType.DMA((3,)),
            pltpu.SemaphoreType.DMA((4, 3)),
            pltpu.SemaphoreType.DMA((3, 64)),
            pltpu.SemaphoreType.DMA((3, 64)),
            pltpu.SemaphoreType.DMA((7, 2, 3)),
        ],
        compiler_params=pltpu.CompilerParams(
            collective_id=0, has_side_effects=True, vmem_limit_bytes=60 * 1024 * 1024
        ),
    )(fwd_idx, bwd_idx, right_sides, inverse_diag, lower_blocks.reshape(3, 4, 512, 128))


def solution(mesh):
    return jax.shard_map(
        on_device,
        mesh=mesh,
        in_specs=(
            P(None, "row", None, None),
            P(None, "row", "col", None),
            P(None, "row", None, "col", None),
            P(),
        ),
        out_specs=P(None, "row", "col", None),
        check_vma=False,
    )
```

time: 212 us -> 188 us (0.89)
  Pallas kernels: 207 us -> 183 us
    pallas_call x1, Pallas kernels: 207 us -> 183 us  [on_device(): pl.pallas_call(kernel, out_shape=jax.ShapeDtypeStruct((4, 4, 32, 128), f3...]
where the time goes in v2:
time: 188 us
  Pallas kernels  183 us (97%)
  local copies, waits for them, and re-layouts  3.8 us (2%)
    pallas_call x1, Pallas kernels, on_device(): pl.pallas_call(kernel, out_shape=jax.ShapeDtypeStruct((4, 4, 32, 128), f3...  183 us

profile of v2, /device:TPU:2, one launch (start us, length us, event | category | flops | bytes accessed | tf_op | source)
XLA Modules:
  0.0 188.0 jit_solution(9774469830637605957)
XLA Ops:
  0.0 0.9 constant_dynamic-slice_fusion
  0.9 0.1 copy.11
  1.0 0.1 reshape.357
  1.1 0.1 copy.10
  1.2 0.1 reshape.356
  1.2 0.1 add_select_fusion.20
  1.3 0.6 select_add_fusion.fwd_idx
  1.9 0.1 select_reduce_fusion.3
  2.1 0.1 select_reduce_fusion.1
  2.2 0.1 copy.12
  2.3 0.8 reshape.358.bwd_idx
  3.1 183.2 %shard_map.46 = f32[4,4,32,128]{3,2,1,0:T(8,128)} custom-call(s32[3,64]{1,0:T(4,128)} %select_add_fusion.fwd_idx, s32[3,512]{1,0:T(4,128)} %reshape.358.bwd_idx, f32[4,4,128,128]{3,2,1,0:T(8,128)} %rhs_hbm.1, f32[4,4,32,128]{3,2,1,0:T(8,128)} %inv_hbm.1, f32[3,4,512,128]{3,2,1,0:T(8,128)} %bitcast.9), custom_call_target="tpu_custom_call" | custom-call | tf_op jit(solution)/shard_map/pallas_call | solution.py:526
  186.3 1.7 copy.14
  (3 shorter events, 0.0 us)

commit v3 on v2

--- a/solution.py
+++ b/solution.py
@@ -7,9 +7,62 @@
 
 MESH = pl.DeviceIdType.MESH
 NZ, NX = 8, 4
-X_POS = {0: 0, 1: 1, 3: 2, 2: 3}
 Z_POS = {0: 0, 1: 1, 7: 2, 2: 3, 6: 4, 3: 5, 5: 6, 4: 7}
-GROUPS = [(0, 1), (1, 2), (3, 2), (5, 2), (7, 1)]
+ROUTES = (
+    (0, 0, 1, 0, 1, 1, ()),
+    (0, 0, -1, 0, 2, 1, ()),
+    (0, 1, 0, 0, 4, 1, ()),
+    (0, -1, 0, 0, 28, 1, ()),
+    (0, 0, 2, 0, 3, 1, ()),
+    (1, 1, 0, 0, 1, 1, ()),
+    (1, -1, 0, 0, 2, 1, ()),
+    (1, 0, -1, 0, 16, 1, ()),
+    (1, 0, 1, 0, 8, 1, ()),
+    (1, 3, 0, 0, 5, 1, ()),
+    (1, -3, 0, 0, 6, 1, ()),
+    (0, 1, 0, 1, 5, 1, (0,)),
+    (0, -1, 0, 1, 29, 1, (0,)),
+    (0, 1, 0, 2, 6, 1, (1,)),
+    (0, -1, 0, 2, 30, 1, (1,)),
+    (0, 1, 0, 4, 8, 1, (2,)),
+    (0, -1, 0, 28, 24, 1, (3,)),
+    (1, 0, 1, 1, 9, 2, (5, 6)),
+    (1, 0, -1, 1, 17, 2, (5, 6)),
+    (0, 1, 0, 3, 7, 1, (4,)),
+    (0, -1, 0, 3, 31, 1, (4,)),
+    (1, 0, 1, 8, 24, 1, (8,)),
+    (1, 1, 0, 1, 3, 1, (5,)),
+    (1, -1, 0, 2, 4, 1, (6,)),
+    (1, 1, 0, 5, 7, 1, (9,)),
+    (0, -1, 0, 29, 25, 1, (12,)),
+    (1, 0, 1, 5, 13, 2, (9, 10)),
+    (1, 0, -1, 5, 21, 2, (9, 10)),
+    (0, 1, 0, 5, 9, 1, (11,)),
+    (0, -1, 0, 30, 26, 1, (14,)),
+    (0, 1, 0, 6, 10, 1, (13,)),
+    (0, -1, 0, 24, 20, 1, (16,)),
+    (0, 1, 0, 8, 12, 1, (15,)),
+    (0, -1, 0, 31, 27, 1, (20,)),
+    (1, 0, -1, 17, 25, 2, (18,)),
+    (0, 2, 0, 8, 16, 1, (15,)),
+    (1, 0, 1, 3, 11, 2, (22, 23)),
+    (1, 0, -1, 3, 19, 2, (22, 23)),
+    (0, -1, 0, 25, 21, 1, (25,)),
+    (0, 1, 0, 7, 11, 1, (19,)),
+    (1, 0, 1, 7, 15, 1, (24,)),
+    (1, 0, -1, 7, 23, 1, (24,)),
+    (0, -1, 0, 26, 22, 1, (29,)),
+    (0, 1, 0, 9, 13, 1, (28,)),
+    (1, 0, -1, 21, 29, 2, (27,)),
+    (0, -2, 0, 26, 18, 1, (29,)),
+    (0, 2, 0, 9, 17, 1, (28,)),
+    (0, -1, 0, 27, 23, 1, (33,)),
+    (0, 1, 0, 10, 14, 1, (30,)),
+    (0, 1, 0, 11, 15, 1, (39,)),
+    (1, 0, 1, 11, 27, 2, (36,)),
+    (0, -2, 0, 27, 19, 1, (33,)),
+    (1, 0, 1, 15, 31, 1, (40,)),
+)
 
 
 def split(v):
@@ -62,6 +115,7 @@
     z_dev = [None] + [at_row((z + a) % NZ, x, core) for a in range(1, NZ)]
     x_rt, x_lf = at_row(z, (x + 1) % NX, core), at_row(z, (x + NX - 1) % NX, core)
     x_far = at_row(z, (x + 2) % NX, core)
+    x_dev = [None, x_rt, x_far, x_lf]
     sib = at_row(z, x, 1 - core)
     col_dev = [None] + [(row, (c + t) % 4) for t in (1, 2, 3)]
 
@@ -75,7 +129,7 @@
         load.start()
 
     barrier = pltpu.get_barrier_semaphore()
-    partners = [z_dev[a] for a in (1, 2, 6, 7)] + [x_rt, x_lf, x_far, sib] + col_dev[1:]
+    partners = [z_dev[a] for a in (1, 2, 3, 5, 6, 7)] + x_dev[1:] + [sib] + col_dev[1:]
     for partner in partners:
         pl.semaphore_signal(barrier, inc=1, device_id=partner, device_id_type=MESH)
 
@@ -106,151 +160,35 @@
 
     def gather_row(level, ready, between):
         g_sem = send_sem.at[0]
-        ids = {}
-
-        def sem(key):
-            return ag_sem.at[level, ids.setdefault(key, len(ids))]
-
-        def ref_a(a, pos, count):
-            return gath[level].at[pl.ds(2 * (a * NX + pos), 2 * count)]
-
-        def ref_b(pos, zpos, count):
-            return gath[level].at[pl.ds(64 + 2 * (pos * NZ + zpos), 2 * count)]
-
-        sib_sem = sem("sib")
-
-        def share(first, count):
-            put(
-                gath[level].at[pl.ds(first, count)], gath[level].at[pl.ds(128 + first, count)],
-                sib_sem, sib, g_sem,
-            )
-
-        def share_a(a, pos, count):
-            share(2 * (a * NX + pos), 2 * count)
-
-        def share_b(pos, zpos, count):
-            share(64 + 2 * (pos * NZ + zpos), 2 * count)
-
-        def z_a(a, p, direction, hops=1):
-            to = (a + direction * hops) % NZ
-            put(ref_a(a, 2 * p, 2), ref_a(to, 2 * p, 2), sem(("az", to, p)), z_dev[direction * hops % NZ], g_sem)
-
-        def x_b(group):
-            zpos, count = GROUPS[group]
-            put(ref_b(0, zpos, count), ref_b(1, zpos, count), sem(("bl", group)), x_rt, g_sem)
-            put(ref_b(0, zpos, count), ref_b(2, zpos, count), sem(("br", group)), x_lf, g_sem)
-
-        def far_b(group):
-            zpos, count = GROUPS[group]
-            if group in (0, 1, 4):
-                put(ref_b(1, zpos, count), ref_b(3, zpos, count), sem(("b2", group)), x_rt, g_sem)
-            else:
-                put(ref_b(2, zpos, count), ref_b(3, zpos, count), sem(("b2", group)), x_lf, g_sem)
-
-        def got_x_b(group):
-            zpos, count = GROUPS[group]
-            if group in (0, 1, 4):
-                take(ref_b(1, zpos, count), sem(("bl", group)))
-                far_b(group)
-                take(ref_b(2, zpos, count), sem(("br", group)))
-            else:
-                take(ref_b(2, zpos, count), sem(("br", group)))
-                far_b(group)
-                take(ref_b(1, zpos, count), sem(("bl", group)))
-            share_b(1, zpos, count)
-            share_b(2, zpos, count)
-
-        def got_far_b(group):
-            zpos, count = GROUPS[group]
-            take(ref_b(3, zpos, count), sem(("b2", group)))
-            share_b(3, zpos, count)
-
-        def z_b(a, hops):
-            to = (a + hops) % NZ
-            put(ref_b(0, Z_POS[a], 1), ref_b(0, Z_POS[to], 1), sem(("bz", to)), z_dev[hops % NZ], g_sem)
-
-        def got_z_b(a):
-            take(ref_b(0, Z_POS[a], 1), sem(("bz", a)))
-            if a == 2:
-                z_b(2, 2)
-                z_b(2, 1)
-            elif a == 6:
-                z_b(6, -1)
-
-        def got_z_a(a, p):
-            take(ref_a(a, 2 * p, 2), sem(("az", a, p)))
-
-        ready(level, 0)
-        gath[level][pl.ds(0, 2)] = fwd[level, pl.ds(0, 2)]
-        put(ref_a(0, 0, 1), ref_a(0, 1, 1), sem("ax1"), x_rt, g_sem)
-        put(ref_a(0, 0, 1), ref_a(0, 3, 1), sem("ax2"), x_far, g_sem)
-        put(ref_a(0, 0, 1), ref_a(0, 2, 1), sem("ax3"), x_lf, g_sem)
-        share_a(0, 0, 1)
-        ready(level, 1)
-        gath[level][pl.ds(64, 2)] = fwd[level, pl.ds(2, 2)]
-        for hops in (2, -2, 1, -1):
-            z_b(0, hops)
-        x_b(0)
-        share_b(0, 0, 1)
+        sib_sem = ag_sem.at[level, 95]
+        issued = set()
+
+        def ref(half, slot, count, plane=0):
+            return gath[level].at[pl.ds(128 * plane + 64 * half + 2 * slot, 2 * count)]
+
+        def share(half, slot, count):
+            put(ref(half, slot, count), ref(half, slot, count, 1), sib_sem, sib, g_sem)
+
+        def issue(arrived, halves):
+            for number, (half, dz, dx, src, dst, count, needs) in enumerate(ROUTES):
+                if number in issued or half not in halves or any(need >= arrived for need in needs):
+                    continue
+                issued.add(number)
+                device = z_dev[dz % NZ] if dz else x_dev[dx % NX]
+                put(ref(half, src, count), ref(half, dst, count), ag_sem.at[level, number], device, g_sem)
+
+        for half in (0, 1):
+            ready(level, half)
+            gath[level][pl.ds(64 * half, 2)] = fwd[level, pl.ds(2 * half, 2)]
+            issue(0, range(half + 1))
+            share(half, 0, 1)
         between()
-        take(ref_a(0, 1, 1), sem("ax1"))
-        z_a(0, 0, 1)
-        z_a(0, 0, -1)
-        take(ref_a(0, 2, 1), sem("ax3"))
-        take(ref_a(0, 3, 1), sem("ax2"))
-        z_a(0, 1, 1)
-        z_a(0, 1, -1)
-        share_a(0, 1, 3)
-        for group, pair in ((1, (1, 7)), (2, (2, 6))):
-            for a in pair:
-                got_z_b(a)
-            x_b(group)
-            share_b(0, *GROUPS[group])
-        got_x_b(0)
-        for p in (0, 1):
-            got_z_a(1, p)
-            z_a(1, p, 1)
-            got_z_a(7, p)
-            z_a(7, p, -1)
-        share_a(1, 0, 4)
-        share_a(7, 0, 4)
-        got_z_b(3)
-        got_z_b(5)
-        x_b(3)
-        share_b(0, *GROUPS[3])
-        got_x_b(1)
-        got_far_b(0)
-        got_z_b(4)
-        x_b(4)
-        share_b(0, *GROUPS[4])
-        got_x_b(2)
-        got_z_a(2, 0)
-        z_a(2, 0, 1, 2)
-        z_a(2, 0, 1)
-        got_z_a(6, 0)
-        z_a(6, 0, -1)
-        got_z_a(6, 1)
-        z_a(6, 1, -1, 2)
-        z_a(6, 1, -1)
-        got_z_a(2, 1)
-        z_a(2, 1, 1)
-        share_a(2, 0, 4)
-        share_a(6, 0, 4)
-        got_far_b(1)
-        got_x_b(3)
-        got_x_b(4)
-        got_far_b(2)
-        for a in (3, 5):
-            got_z_a(a, 0)
-            got_z_a(a, 1)
-            share_a(a, 0, 4)
-        got_far_b(3)
-        got_far_b(4)
-        got_z_a(4, 0)
-        got_z_a(4, 1)
-        share_a(4, 0, 4)
+        for number, (half, dz, dx, src, dst, count, needs) in enumerate(ROUTES):
+            take(ref(half, dst, count), ag_sem.at[level, number])
+            issue(number + 1, (0, 1))
+            share(half, dst, count)
         take(gath[level].at[pl.ds(128, 128)], sib_sem)
-        sent(252, g_sem)
+        sent(2 * sum(route[5] for route in ROUTES) + 128, g_sem)
 
     def reduce_row(low_level, build):
         r_sem = send_sem.at[0]
@@ -404,7 +342,7 @@
         for half in (0, 1):
             for j in (2 * half, 2 * half + 1):
                 picked = jnp.concatenate(
-                    [gath[low_level][fwd_idx[low_level, 16 * j + d]] for d in range(16)], axis=0
+                    [gath[low_level][fwd_idx[low_level, 4 * core + j, d]] for d in range(16)], axis=0
                 )
                 update = split_dot((low_hi[j], low_lo[j]), split(picked))
                 done = exact_dot(inv[level, j].reshape(128, 128), update)
@@ -468,15 +406,15 @@
 
         def build_mine(place, inner):
             own[low_level, place] = (
-                terms[low_level][bwd_idx[low_level, 4 * place]]
-                + terms[low_level][bwd_idx[low_level, 4 * place + 1]]
+                terms[low_level][bwd_idx[low_level, place]]
+                + terms[low_level][bwd_idx[low_level, 128 + place]]
             )
             return inner
 
         def build_other(place, inner):
             own[low_level, place] += (
-                others[low_level][bwd_idx[low_level, 4 * place + 2]]
-                + others[low_level][bwd_idx[low_level, 4 * place + 3]]
+                others[low_level][bwd_idx[low_level, 256 + place]]
+                + others[low_level][bwd_idx[low_level, 384 + place]]
             )
             return inner
 
@@ -499,21 +437,22 @@
 def on_device(right_sides, inverse_diag, lower_blocks, depends_on):
     row = lax.axis_index("row")
     z, x, core = row // (2 * NX), row // 2 % NX, row % 2
-    mine = lax.dynamic_slice(depends_on, (0, 4 * row, 0), (3, 4, 16)).reshape(3, 64)
-    other = lax.dynamic_slice(depends_on, (0, 4 * (row + 1 - 2 * core), 0), (3, 4, 16)).reshape(3, 64)
-    place, owner_core = block_place(mine, lambda zz: z - zz, lambda xx: x - xx)
+    wanted = lax.dynamic_slice(depends_on, (0, 4 * (row - core), 0), (3, 8, 16))
+    place, owner_core = block_place(wanted, lambda zz: z - zz, lambda xx: x - xx)
     fwd_idx = place + jnp.where(owner_core == core, 0, 128)
+    place, owner_core = block_place(wanted, lambda zz: zz - z, lambda xx: xx - x)
+    place = jnp.where(owner_core == core, place, -1)
+    match = place[:, :, :, None] == jnp.arange(128, dtype=jnp.int32)
+    entry = 16 * (jnp.arange(8, dtype=jnp.int32) % 4)[:, None] + jnp.arange(16, dtype=jnp.int32)
+    owner = (jnp.arange(8, dtype=jnp.int32) // 4)[:, None]
     lists = []
-    for wanted in (mine, other):
-        place, owner_core = block_place(wanted, lambda zz: zz - z, lambda xx: xx - x)
-        place = jnp.where(owner_core == core, place, -1)
-        match = place[:, None, :] == jnp.arange(128, dtype=jnp.int32)[None, :, None]
-        entry = jnp.arange(64, dtype=jnp.int32)[None, None, :]
-        first = jnp.min(jnp.where(match, entry, 64), axis=2)
-        last = jnp.max(jnp.where(match, entry, -1), axis=2)
+    for source in (core, 1 - core):
+        found = match & (owner == source)[:, :, None]
+        first = jnp.min(jnp.where(found, entry[:, :, None], 64), axis=(1, 2))
+        last = jnp.max(jnp.where(found, entry[:, :, None], -1), axis=(1, 2))
         lists.append(first)
         lists.append(jnp.where(last > first, last, 64))
-    bwd_idx = jnp.stack(lists, axis=2).reshape(3, 512)
+    bwd_idx = jnp.concatenate(lists, axis=1)
 
     f32 = jnp.float32
 
@@ -563,7 +502,7 @@
             pltpu.SemaphoreType.DMA((4,)),
             pltpu.SemaphoreType.DMA((3,)),
             pltpu.SemaphoreType.DMA((4, 3)),
-            pltpu.SemaphoreType.DMA((3, 64)),
+            pltpu.SemaphoreType.DMA((3, 96)),
             pltpu.SemaphoreType.DMA((3, 64)),
             pltpu.SemaphoreType.DMA((7, 2, 3)),
         ],

time: 188 us -> 186 us (0.989)
  no operation moved by 1% of the time
where the time goes in v3:
time: 186 us
  Pallas kernels  182 us (98%)
  local copies, waits for them, and re-layouts  2.51 us (1%)
    pallas_call x1, Pallas kernels, on_device(): pl.pallas_call(kernel, out_shape=jax.ShapeDtypeStruct((4, 4, 32, 128), f3...  182 us

profile of v3, /device:TPU:2, one launch (start us, length us, event | category | flops | bytes accessed | tf_op | source)
XLA Modules:
  0.0 185.9 jit_solution(4407228617566760830)
XLA Ops:
  0.0 0.0 copy-start
  0.0 0.1 iota_add_fusion
  0.1 0.7 copy-done
  0.8 0.1 constant_dynamic-slice_fusion
  0.9 0.1 copy.7
  0.9 0.7 add_select_fusion.11
  1.6 0.2 select_reduce_fusion.3
  1.9 0.6 pad_add_fusion.bwd_idx
  2.5 181.7 %shard_map.46 = f32[4,4,32,128]{3,2,1,0:T(8,128)} custom-call(s32[3,8,16]{2,1,0:T(8,128)} %get-tuple-element.12.fwd_idx, s32[3,512]{1,0:T(4,128)} %pad_add_fusion.bwd_idx, f32[4,4,128,128]{3,2,1,0:T(8,128)} %rhs_hbm.1, f32[4,4,32,128]{3,2,1,0:T(8,128)} %inv_hbm.1, f32[3,4,512,128]{3,2,1,0:T(8,128)} %bitcast.1), custom_call_target="tpu_custom_call" | custom-call | tf_op jit(solution)/shard_map/pallas_call | solution.py:465
  184.2 1.7 copy.9
  (4 shorter events, 0.0 us)
Async XLA Ops:
  0.0 0.8 copy-start

commit v4 on v3

--- a/solution.py
+++ b/solution.py
@@ -198,7 +198,7 @@
             return rs_sem.at[low_level, ids.setdefault(key, len(ids))]
 
         def own_a(a, p):
-            return own.at[low_level, pl.ds(2 * (a * NX + 2 * p), 4)]
+            return own.at[low_level, pl.ds(2 * (a * NX + p), 2)]
 
         def own_b(pos, zpos, count):
             return own.at[low_level, pl.ds(64 + 2 * (pos * NZ + zpos), 2 * count)]
@@ -213,7 +213,7 @@
         def pass_az(hops, p, direction):
             ref = ref_az(hops, p, direction)
             take(ref, sem(("az", hops, p, direction)))
-            if hops == 2 and p == (0 if direction == 1 else 1):
+            if hops == 2 and (p < 2) == (direction == 1):
                 far = ref_az(3, p, direction)
                 take(far, sem(("az", 3, p, direction)))
                 ref[...] += own_a(direction * hops % NZ, p)[...] + far[...]
@@ -233,12 +233,10 @@
         put(own_b(3, 3, 4), mid(mid_r, 1), sem(("m", 1)), x_lf, r_sem)
         put(own_b(3, 0, 3), mid(mid_l, 2), sem(("m", 2)), x_rt, r_sem)
         build(24, 24)
-        send_az(own_a(4, 0), 4, 0, 1, 2)
-        send_az(own_a(4, 1), 4, 1, -1, 2)
-        send_az(own_a(3, 0), 3, 0, 1)
-        send_az(own_a(5, 1), 3, 1, -1)
-        send_az(own_a(3, 1), 3, 1, 1)
-        send_az(own_a(5, 0), 3, 0, -1)
+        for p in (3, 1, 2, 0):
+            send_az(own_a(4, p), 4, p, 1 if p < 2 else -1, 2)
+            send_az(own_a(3, p), 3, p, 1)
+            send_az(own_a(5, p), 3, p, -1)
         build(80, 32)
         put(own_b(2, 7, 1), mid(fin_r, 0), sem(("fr", 0)), x_lf, r_sem)
         put(own_b(1, 3, 4), mid(fin_l, 1), sem(("fl", 1)), x_rt, r_sem)
@@ -252,13 +250,15 @@
         take(mid(mid_r, 1), sem(("m", 1)))
         mid(mid_r, 1)[...] += own_b(2, 3, 4)[...]
         put(mid(mid_r, 1), mid(fin_r, 1), sem(("fr", 1)), x_lf, r_sem)
-        pass_az(2, 1, 1)
-        pass_az(2, 0, -1)
+        for p in (3, 1):
+            pass_az(2, p, 1)
+            pass_az(2, p, -1)
         take(mid(mid_l, 2), sem(("m", 2)))
         mid(mid_l, 2)[...] += own_b(1, 0, 3)[...]
         put(mid(mid_l, 2), mid(fin_l, 2), sem(("fl", 2)), x_rt, r_sem)
-        pass_az(2, 0, 1)
-        pass_az(2, 1, -1)
+        for p in (2, 0):
+            pass_az(2, p, 1)
+            pass_az(2, p, -1)
 
         def finish_x(part_no):
             zpos, count = zs[part_no]
@@ -280,37 +280,37 @@
 
         finish_x(0)
         send_bz(z_part(4), 0, 2)
-        pass_az(1, 1, 1)
-        pass_az(1, 0, -1)
+        for p in (3, 1):
+            pass_az(1, p, 1)
+            pass_az(1, p, -1)
         finish_x(1)
         send_bz(z_part(3), 1, 1)
         send_bz(z_part(5), 2, -1)
-        pass_az(1, 0, 1)
-        pass_az(1, 1, -1)
         finish_x(2)
         send_bz(z_part(1), 5, 1)
         send_bz(z_part(7), 6, -1)
+        for p in (2, 0):
+            pass_az(1, p, 1)
+            pass_az(1, p, -1)
         z_part(2)[...] += got_bz(0) + got_bz(1)
         send_bz(z_part(2), 3, 2)
         z_part(6)[...] += got_bz(2)
         send_bz(z_part(6), 4, -2)
-        for p in (1, 0):
+        for p in (3, 1, 2, 0):
             pass_az(0, p, 1)
             pass_az(0, p, -1)
             row_x[low_level, p] = own_a(0, p)[...] + up_a[low_level, 0, p] + dn_a[low_level, 0, p]
-            if p == 1:
-                put(row_x.at[low_level, 1, pl.ds(2, 2)], in_x.at[low_level, 2], sem("x3"), x_far, r_sem)
-                put(row_x.at[low_level, 1, pl.ds(0, 2)], in_x.at[low_level, 1], sem("x2"), x_lf, r_sem)
-            else:
-                put(row_x.at[low_level, 0, pl.ds(2, 2)], in_x.at[low_level, 0], sem("x1"), x_rt, r_sem)
+            if p:
+                device = (None, x_rt, x_lf, x_far)[p]
+                put(row_x.at[low_level, p], in_x.at[low_level, p - 1], sem(("x", p)), device, r_sem)
         half_b = col_z[low_level, pl.ds(0, 2)]
         for key in (5, 6, 3, 4):
             half_b = half_b + got_bz(key)
         start_solve(low_level, 1, fwd[low_level, pl.ds(2, 2)] - half_b)
-        for slot in (2, 1, 0):
-            take(in_x.at[low_level, slot], sem("x%d" % (slot + 1)))
+        for p in (1, 3, 2):
+            take(in_x.at[low_level, p - 1], sem(("x", p)))
         half_a = (
-            row_x[low_level, 0, pl.ds(0, 2)] + in_x[low_level, 0] + in_x[low_level, 1] + in_x[low_level, 2]
+            row_x[low_level, 0] + in_x[low_level, 0] + in_x[low_level, 1] + in_x[low_level, 2]
         )
         start_solve(low_level, 0, fwd[low_level, pl.ds(0, 2)] - half_a)
         sent(188, r_sem)
@@ -391,7 +391,7 @@
         start_solve(3, half, fwd[3, pl.ds(2 * half, 2)])
 
     def backward_level(low_level):
-        t_sem = rs_sem.at[low_level, 63]
+        t_sem = rs_sem.at[low_level, 95]
 
         def product(j):
             value = exact_dot(low[low_level, j], sol[j])
@@ -489,9 +489,9 @@
             vmem(65, *block),
             vmem(65, *block),
             vmem(3, 128, *block),
-            vmem(3, 4, 2, 4, *block),
-            vmem(3, 4, 2, 4, *block),
-            vmem(3, 2, 4, *block),
+            vmem(3, 4, 4, 2, *block),
+            vmem(3, 4, 4, 2, *block),
+            vmem(3, 4, 2, *block),
             vmem(3, 3, 2, *block),
             vmem(3, 16, *block),
             vmem(3, 16, *block),
@@ -503,7 +503,7 @@
             pltpu.SemaphoreType.DMA((3,)),
             pltpu.SemaphoreType.DMA((4, 3)),
             pltpu.SemaphoreType.DMA((3, 96)),
-            pltpu.SemaphoreType.DMA((3, 64)),
+            pltpu.SemaphoreType.DMA((3, 96)),
             pltpu.SemaphoreType.DMA((7, 2, 3)),
         ],
         compiler_params=pltpu.CompilerParams(

time: 186 us -> 181 us (0.973)
  Pallas kernels: 182 us -> 177 us
    pallas_call x1, Pallas kernels: 182 us -> 177 us  [on_device(): pl.pallas_call(kernel, out_shape=jax.ShapeDtypeStruct((4, 4, 32, 128), f3...]
where the time goes in v4:
time: 181 us
  Pallas kernels  177 us (98%)
  local copies, waits for them, and re-layouts  2.51 us (1%)
    pallas_call x1, Pallas kernels, on_device(): pl.pallas_call(kernel, out_shape=jax.ShapeDtypeStruct((4, 4, 32, 128), f3...  177 us

profile of v4, /device:TPU:2, one launch (start us, length us, event | category | flops | bytes accessed | tf_op | source)
XLA Modules:
  0.0 180.7 jit_solution(17491241283221160862)
XLA Ops:
  0.0 0.0 copy-start
  0.0 0.1 iota_add_fusion
  0.1 0.7 copy-done
  0.8 0.1 constant_dynamic-slice_fusion
  0.9 0.1 copy.7
  0.9 0.7 add_select_fusion.11
  1.6 0.2 select_reduce_fusion.3
  1.9 0.6 pad_add_fusion.bwd_idx
  2.5 176.6 %shard_map.46 = f32[4,4,32,128]{3,2,1,0:T(8,128)} custom-call(s32[3,8,16]{2,1,0:T(8,128)} %get-tuple-element.12.fwd_idx, s32[3,512]{1,0:T(4,128)} %pad_add_fusion.bwd_idx, f32[4,4,128,128]{3,2,1,0:T(8,128)} %rhs_hbm.1, f32[4,4,32,128]{3,2,1,0:T(8,128)} %inv_hbm.1, f32[3,4,512,128]{3,2,1,0:T(8,128)} %bitcast.1), custom_call_target="tpu_custom_call" | custom-call | tf_op jit(solution)/shard_map/pallas_call | solution.py:465
  179.0 1.7 copy.9
  (4 shorter events, 0.0 us)
Async XLA Ops:
  0.0 0.8 copy-start

commit v5 on v4

--- a/solution.py
+++ b/solution.py
@@ -159,7 +159,7 @@
         ).wait_send()
 
     def gather_row(level, ready, between):
-        g_sem = send_sem.at[0]
+        g_sem = send_sem.at[level]
         sib_sem = ag_sem.at[level, 95]
         issued = set()
 
@@ -188,10 +188,9 @@
             issue(number + 1, (0, 1))
             share(half, dst, count)
         take(gath[level].at[pl.ds(128, 128)], sib_sem)
-        sent(2 * sum(route[5] for route in ROUTES) + 128, g_sem)
 
     def reduce_row(low_level, build):
-        r_sem = send_sem.at[0]
+        r_sem = send_sem.at[3 + low_level]
         ids = {}
 
         def sem(key):
@@ -313,12 +312,11 @@
             row_x[low_level, 0] + in_x[low_level, 0] + in_x[low_level, 1] + in_x[low_level, 2]
         )
         start_solve(low_level, 0, fwd[low_level, pl.ds(0, 2)] - half_a)
-        sent(188, r_sem)
 
     for level in (1, 2, 3, 0):
         for t in (1, 2, 3):
             ref = inv.at[level, :, c]
-            put(ref, ref, inv_sem.at[level, t - 1], col_dev[t], send_sem.at[1])
+            put(ref, ref, inv_sem.at[level, t - 1], col_dev[t], send_sem.at[6])
 
     def whole_inv(level):
         for t in (1, 2, 3):
@@ -352,7 +350,7 @@
                 put(
                     part.at[low_level, (c + t) % 4, pl.ds(2 * half, 2)],
                     col_in.at[low_level, t - 1, pl.ds(2 * half, 2)],
-                    col_sem.at[low_level, half, t - 1], col_dev[t], send_sem.at[2],
+                    col_sem.at[low_level, half, t - 1], col_dev[t], send_sem.at[7],
                 )
 
     def finish_forward(level, half):
@@ -374,7 +372,7 @@
         rest[level, c, blocks] = value
         ref = rest.at[level, c, blocks]
         for t in (2, 1, 3):
-            put(ref, ref, col_sem.at[3 + level, half, t - 1], col_dev[t], send_sem.at[2])
+            put(ref, ref, col_sem.at[3 + level, half, t - 1], col_dev[t], send_sem.at[7])
 
     def finish_solve(level, half, product):
         blocks = pl.ds(2 * half, 2)
@@ -398,7 +396,7 @@
             terms[low_level][pl.ds(16 * j, 16)] = value.reshape(16, 32, 128)
             put(
                 terms[low_level].at[pl.ds(16 * j, 16)], others[low_level].at[pl.ds(16 * j, 16)],
-                t_sem, sib, send_sem.at[0],
+                t_sem, sib, send_sem.at[3 + low_level],
             )
 
         finish_solve(low_level + 1, 1, product)
@@ -430,8 +428,11 @@
         backward_level(low_level)
     for half in (1, 0):
         finish_solve(0, half, lambda j: None)
-    sent(48, send_sem.at[1])
-    sent(84, send_sem.at[2])
+    sent(48, send_sem.at[6])
+    sent(84, send_sem.at[7])
+    for level in range(3):
+        sent(2 * sum(route[5] for route in ROUTES) + 128, send_sem.at[level])
+        sent(188, send_sem.at[3 + level])
 
 
 def on_device(right_sides, inverse_diag, lower_blocks, depends_on):
@@ -500,7 +501,7 @@
             vmem(3, 16, *block),
             vmem(3, 7, 2, *block),
             pltpu.SemaphoreType.DMA((4,)),
-            pltpu.SemaphoreType.DMA((3,)),
+            pltpu.SemaphoreType.DMA((8,)),
             pltpu.SemaphoreType.DMA((4, 3)),
             pltpu.SemaphoreType.DMA((3, 96)),
             pltpu.SemaphoreType.DMA((3, 96)),

time: 181 us -> 179 us (0.989)
  Pallas kernels: 177 us -> 175 us
where the time goes in v5:
time: 179 us
  Pallas kernels  175 us (98%)
  local copies, waits for them, and re-layouts  2.51 us (1%)
    pallas_call x1, Pallas kernels, on_device(): pl.pallas_call(kernel, out_shape=jax.ShapeDtypeStruct((4, 4, 32, 128), f3...  175 us

profile of v5, /device:TPU:2, one launch (start us, length us, event | category | flops | bytes accessed | tf_op | source)
XLA Modules:
  0.0 178.9 jit_solution(2612970022050093091)
XLA Ops:
  0.0 0.0 copy-start
  0.0 0.1 iota_add_fusion
  0.1 0.7 copy-done
  0.8 0.1 constant_dynamic-slice_fusion
  0.9 0.1 copy.7
  0.9 0.7 add_select_fusion.11
  1.6 0.2 select_reduce_fusion.3
  1.9 0.6 pad_add_fusion.bwd_idx
  2.5 174.8 %shard_map.46 = f32[4,4,32,128]{3,2,1,0:T(8,128)} custom-call(s32[3,8,16]{2,1,0:T(8,128)} %get-tuple-element.12.fwd_idx, s32[3,512]{1,0:T(4,128)} %pad_add_fusion.bwd_idx, f32[4,4,128,128]{3,2,1,0:T(8,128)} %rhs_hbm.1, f32[4,4,32,128]{3,2,1,0:T(8,128)} %inv_hbm.1, f32[3,4,512,128]{3,2,1,0:T(8,128)} %bitcast.1), custom_call_target="tpu_custom_call" | custom-call | tf_op jit(solution)/shard_map/pallas_call | solution.py:466
  177.3 1.7 copy.9
  (4 shorter events, 0.0 us)
Async XLA Ops:
  0.0 0.8 copy-start
